TPU v7x, 1024 devices: a whole 8x8x8 slice. The times are simulated.
1024 devices in a mesh: gx: 128 (over x, y, core), gy: 8 (over z).
Axes of the slice: x: 8, y: 8, z: 8, core: 2. Of those that a mesh axis runs over, the one named last changes fastest.
Arguments:
- concentration: float32 [512, 512, 128], P('gx', 'gy'), may hold values from -4 to 4
- potential: float32 [512, 512, 128], P('gx', 'gy'), may hold values from -4 to 4
- mass_source: float32 [512, 512, 128], P('gx', 'gy'), may hold values from -7 to 7
- potential_source: float32 [512, 512, 128], P('gx', 'gy'), may hold values from -7 to 7
- pore_mask: int32 [512, 512, 128], P('gx', 'gy'), may hold values 0 or 1
- mobility_class: int32 [512, 512, 128], P('gx', 'gy'), may hold values from 0 to 7
- mobility_table: float32 [8], replicated, may hold values from 0.05 to 1
- owner_map: int32 [128, 512], P(None, 'gy'), may hold values from 0 to 127, as said below
Outputs:
- conc_out: float32 [512, 512, 128], P('gx', 'gy')
- pot_out: float32 [512, 512, 128], P('gx', 'gy')
Inputs may be any that keep to these rules, and one draw needn't show every extreme that they name: `owner_map`: no owner is named by more than 2 entries of one device; in every draw, for each gy index, one owner is named by exactly 2 entries of every device of that gy index.
All inputs are finite; a program needn't handle non-finite values. No bound on the sum of `pore_mask` on one device may be relied on, other than what follows from the above.
Results may differ from a plain program's by a relative error of at most 0.000058.
Values sent between devices are 32-bit elements; how exact they have to be, the bound alone decides.
A program may use at most 32 MiB of HBM per device.

v0:
```python
import jax
import jax.numpy as jnp
from jax import lax
from jax.sharding import PartitionSpec as P

NCLASS = 8
CSWEEP = 3


time_step = 0.25
split_slope = 1.0
interface = 0.5
relax_fine = 0.6
relax_coarse = 0.6
coarse_flux = 0.0625
coarse_bend = 0.125
coarse_det = 1.0 + 2.0 * coarse_flux * (split_slope + 2.0 * coarse_bend)


def with_halo(cells, sides, width):
    for axis, dim in sides:
        count = lax.axis_size(axis)
        ends = count - 1
        head = lax.slice_in_dim(cells, 0, width, axis=dim)
        tail = lax.slice_in_dim(cells, cells.shape[dim] - width, cells.shape[dim], axis=dim)
        cells = jnp.concatenate(
            [
                lax.ppermute(tail, axis, [(i, (i + 1) % count) for i in range(ends)]),
                cells,
                lax.ppermute(head, axis, [((i + 1) % count, i) for i in range(ends)]),
            ],
            axis=dim,
        )
    return cells


def lookup_mobility(pore_mask, mobility_class, mobility_table):
    values = jnp.zeros(mobility_class.shape, jnp.float32)
    for class_marker in range(NCLASS):
        values = jnp.where(mobility_class == class_marker, mobility_table[class_marker], values)
    return pore_mask.astype(jnp.float32) * values


def neighbours(padded):
    center = padded[1:-1, 1:-1, :]
    along_planes = jnp.pad(center, ((0, 0), (0, 0), (1, 1)))
    return (
        padded[2:, 1:-1, :],
        padded[:-2, 1:-1, :],
        padded[1:-1, 2:, :],
        padded[1:-1, :-2, :],
        along_planes[:, :, 2:],
        along_planes[:, :, :-2],
    )


def face_terms(padded_mobility):
    center = padded_mobility[1:-1, 1:-1, :]
    return tuple((0.5 * (center + other) for other in neighbours(padded_mobility)))


def residuals(padded_conc, padded_pot, faces, mass_source, potential_source):
    conc_now = padded_conc[1:-1, 1:-1, :]
    pot_now = padded_pot[1:-1, 1:-1, :]
    flux = jnp.zeros_like(pot_now)
    for face, other in zip(faces, neighbours(padded_pot)):
        flux = flux + face * (other - pot_now)
    laplace = -6.0 * conc_now
    for other in neighbours(padded_conc):
        laplace = laplace + other
    excess_mass = mass_source - (conc_now - time_step * flux)
    excess_pot = potential_source - (pot_now - split_slope * conc_now + interface * laplace)
    return (excess_mass, excess_pot)


def relax_pair(conc_now, pot_now, excess_mass, excess_pot, diagonal):
    other_diagonal = -(split_slope + 6.0 * interface)
    determinant = 1.0 - diagonal * other_diagonal
    new_conc = conc_now + relax_fine * (excess_mass - diagonal * excess_pot) / determinant
    new_pot = pot_now + relax_fine * (excess_pot - other_diagonal * excess_mass) / determinant
    return (new_conc, new_pot)


def restrict(field):
    size_x, size_y, size_p = field.shape
    return field.reshape(size_x // 2, 2, size_y // 2, 2, size_p // 2, 2).sum(axis=(1, 3, 5)) / 8.0


def prolong(coarse):
    size_x, size_y, size_p = coarse.shape
    wide = jnp.broadcast_to(coarse[:, None, :, None, :, None], (size_x, 2, size_y, 2, size_p, 2))
    return wide.reshape(2 * size_x, 2 * size_y, 2 * size_p)


def neighbour_sum(values):
    padded = jnp.pad(values, [(0, 0)] * (values.ndim - 1) + [(1, 1)])
    return padded[..., 2:] + padded[..., :-2]


def coarse_solve(mean):
    half_planes = mean.shape[-1] // 2
    mass_mean = mean[..., :half_planes]
    pot_mean = mean[..., half_planes:]
    coarse_conc = jnp.zeros_like(mass_mean)
    coarse_pot = jnp.zeros_like(pot_mean)
    for pass_index in range(CSWEEP):
        mass_gap = mass_mean - (
            coarse_conc + coarse_flux * (2.0 * coarse_pot - neighbour_sum(coarse_pot))
        )
        pot_gap = pot_mean - (
            coarse_pot
            - split_slope * coarse_conc
            + coarse_bend * (neighbour_sum(coarse_conc) - 2.0 * coarse_conc)
        )
        coarse_conc = (
            coarse_conc + relax_coarse * (mass_gap - 2.0 * coarse_flux * pot_gap) / coarse_det
        )
        coarse_pot = (
            coarse_pot
            + relax_coarse * (pot_gap + (split_slope + 2.0 * coarse_bend) * mass_gap) / coarse_det
        )
    return jnp.concatenate([coarse_conc, coarse_pot], axis=-1)


def on_device(
    concentration,
    potential,
    mass_source,
    potential_source,
    pore_mask,
    mobility_class,
    mobility_table,
    owner_map,
):
    mobility = lookup_mobility(pore_mask, mobility_class, mobility_table)
    padded_mobility = with_halo(mobility, (("gx", 0), ("gy", 1)), 1)
    faces = face_terms(padded_mobility)
    diagonal = jnp.zeros_like(mobility)
    for face in faces:
        diagonal = diagonal + face
    diagonal = time_step * diagonal

    def excess_of(conc_now, pot_now):
        padded = with_halo(jnp.stack([conc_now, pot_now]), (("gx", 1), ("gy", 2)), 1)
        return residuals(padded[0], padded[1], faces, mass_source, potential_source)

    conc_now, pot_now = (concentration, potential)
    excess_mass, excess_pot = excess_of(conc_now, pot_now)
    conc_now, pot_now = relax_pair(conc_now, pot_now, excess_mass, excess_pot, diagonal)
    excess_mass, excess_pot = excess_of(conc_now, pot_now)
    blocks = jnp.concatenate([restrict(excess_mass), restrict(excess_pot)], axis=-1)
    coarse_x, coarse_y, planes = blocks.shape
    columns = coarse_x * coarse_y
    blocks = blocks.reshape(columns, planes)
    groups = lax.axis_size("gx")
    capacity = max(2, 2 * columns // groups)
    my_index = lax.axis_index("gx")
    owner = lax.dynamic_slice_in_dim(owner_map, my_index, 1, 0)[0]
    member_count = jnp.sum((owner_map == my_index).astype(jnp.float32))
    count_floor = jnp.maximum(member_count, 1.0)
    member = owner[:, None] == jnp.arange(groups, dtype=jnp.int32)[None, :]
    member_integer = member.astype(jnp.int32)
    earlier = (jnp.arange(columns)[:, None] > jnp.arange(columns)[None, :]).astype(jnp.int32)
    before = jnp.dot(earlier, member_integer)
    rank = jnp.sum(before * member_integer, axis=1)
    slot = owner * capacity + rank
    placing = (jnp.arange(groups * capacity, dtype=jnp.int32)[:, None] == slot[None, :]).astype(
        jnp.float32
    )
    outgoing = jnp.dot(placing, blocks, precision=lax.Precision.HIGHEST).reshape(
        groups, capacity, planes
    )
    incoming = lax.all_to_all(outgoing, "gx", split_axis=0, concat_axis=0, tiled=True)
    own_part = coarse_solve(jnp.sum(incoming, axis=(0, 1)) / count_floor)
    reply = jnp.broadcast_to(own_part, (groups, capacity, planes))
    returned = lax.all_to_all(reply, "gx", split_axis=0, concat_axis=0, tiled=True)
    correction = jnp.dot(
        placing.T, returned.reshape(groups * capacity, planes), precision=lax.Precision.HIGHEST
    )
    correction = correction.reshape(coarse_x, coarse_y, planes)
    half_planes = planes // 2
    conc_now = conc_now + prolong(correction[..., :half_planes])
    pot_now = pot_now + prolong(correction[..., half_planes:])
    excess_mass, excess_pot = excess_of(conc_now, pot_now)
    conc_now, pot_now = relax_pair(conc_now, pot_now, excess_mass, excess_pot, diagonal)
    return (conc_now, pot_now)


def solution(mesh):
    in_specs = (
        P("gx", "gy", None),
        P("gx", "gy", None),
        P("gx", "gy", None),
        P("gx", "gy", None),
        P("gx", "gy", None),
        P("gx", "gy", None),
        P(),
        P(None, "gy"),
    )
    out_specs = (P("gx", "gy", None), P("gx", "gy", None))
    return jax.shard_map(
        on_device, mesh=mesh, in_specs=in_specs, out_specs=out_specs, check_vma=False
    )
```

profile of v0, /device:TPU:1, one launch (start us, length us, event | category | flops | bytes accessed | tf_op | source)
XLA Modules:
  0.0 185.9 jit_solution(10153466057767341714)
XLA Ops:
  0.7 1.6 fusion.95
  2.3 6.2 %select_multiply_fusion = f32[4,64,128]{2,1,0:T(8,128)S(1)} fusion(s32[4,64,128]{2,1,0:T(8,128)} %param.12, s32[4,64,128]{2,1,0:T(8,128)} %param.13, f32[]{:T(128)} %bitcast.10, f32[]{:T(128)} %bitcast.9, f32[]{:T(128)} %bitcast.8, f32[]{:T(128)} %bitcast.7, f32[]{:T(128)} %bitcast.6, f32[]{:T(128)} %bitcast.5, f32[]{:T(128)} %bitcast.4, f32[]{:T(128)} %bitcast.3), kind=kLoop, calls=%fused_computation.138 | loop fusion | flops 589824 | bytes 393248 | tf_op jit(solution)/shard_map/mul | solution.py:41
  8.5 16.1 %collective-permute-start.4 = (f32[1,64,128]{2,1,0:T(8,128)S(1)}, f32[1,64,128]{2,1,0:T(8,128)S(1)}, u32[]{:S(2)}, u32[]{:S(2)}) collective-permute-start(f32[1,64,128]{2,1,0:T(8,128)S(1)} %get-tuple-element.43), channel_id=1, source_target_pairs={{8,0},{16,8},{24,16},{32,24},{40,32},{48,40},{56,48},{64,56},{72,6... | collective-permute-start | bytes 98312 | tf_op jit(solution)/shard_map/ppermute | solution.py:30
  24.6 1.9 %collective-permute-start.5 = (f32[1,64,128]{2,1,0:T(8,128)S(1)}, f32[1,64,128]{2,1,0:T(8,128)S(1)}, u32[]{:S(2)}, u32[]{:S(2)}) collective-permute-start(f32[1,64,128]{2,1,0:T(8,128)S(1)} %get-tuple-element.42), channel_id=1, source_target_pairs={{0,8},{8,16},{16,24},{24,32},{32,40},{40,48},{48,56},{56,64},{64,7... | collective-permute-start | bytes 98312 | tf_op jit(solution)/shard_map/ppermute | solution.py:28
  27.3 1.9 %collective-permute-start = (f32[2,1,64,128]{3,2,1,0:T(8,128)S(1)}, f32[2,1,64,128]{3,2,1,0:T(8,128)S(1)}, u32[]{:S(2)}, u32[]{:S(2)}) collective-permute-start(f32[2,1,64,128]{3,2,1,0:T(8,128)S(1)} %get-tuple-element.36), channel_id=1, source_target_pairs={{0,8},{8,16},{16,24},{24,32},{32,40},{40,48},{48,56},{56,64},{64,7... | collective-permute-start | bytes 196616 | tf_op jit(solution)/shard_map/ppermute | solution.py:28
  29.2 2.4 %collective-permute-start.1 = (f32[2,1,64,128]{3,2,1,0:T(8,128)S(1)}, f32[2,1,64,128]{3,2,1,0:T(8,128)S(1)}, u32[]{:S(2)}, u32[]{:S(2)}) collective-permute-start(f32[2,1,64,128]{3,2,1,0:T(8,128)S(1)} %get-tuple-element.37), channel_id=1, source_target_pairs={{8,0},{16,8},{24,16},{32,24},{40,32},{48,40},{56,48},{64,56},{72,6... | collective-permute-start | bytes 196616 | tf_op jit(solution)/shard_map/ppermute | solution.py:30
  32.9 1.9 %collective-permute-done.1 = f32[2,1,64,128]{3,2,1,0:T(8,128)S(1)} collective-permute-done((f32[2,1,64,128]{3,2,1,0:T(8,128)S(1)}, f32[2,1,64,128]{3,2,1,0:T(8,128)S(1)}, u32[]{:S(2)}, u32[]{:S(2)}) %collective-permute-start.1) | collective-permute-done | bytes 65568 | tf_op jit(solution)/shard_map/ppermute | solution.py:30
  39.5 4.6 %collective-permute-start.7 = (f32[6,1,128]{2,1,0:T(1,128)S(1)}, f32[6,1,128]{2,1,0:T(1,128)S(1)}, u32[]{:S(2)}, u32[]{:S(2)}) collective-permute-start(f32[6,1,128]{2,1,0:T(1,128)S(1)} %get-tuple-element.41), channel_id=1, source_target_pairs={{0,1},{1,2},{2,3},{3,4},{4,5},{5,6},{6,7},{8,9},{9,10},{10,11},{11... | collective-permute-start | bytes 9224 | tf_op jit(solution)/shard_map/ppermute | solution.py:28
  45.3 1.4 divide_add_fusion.2
  47.7 2.6 %collective-permute-start.8 = (f32[2,1,64,128]{3,2,1,0:T(8,128)S(1)}, f32[2,1,64,128]{3,2,1,0:T(8,128)S(1)}, u32[]{:S(2)}, u32[]{:S(2)}) collective-permute-start(f32[2,1,64,128]{3,2,1,0:T(8,128)S(1)} %get-tuple-element.34), channel_id=1, source_target_pairs={{0,8},{8,16},{16,24},{24,32},{32,40},{40,48},{48,56},{56,64},{64,7... | collective-permute-start | bytes 196616 | tf_op jit(solution)/shard_map/ppermute | solution.py:28
  50.3 1.9 %collective-permute-start.9 = (f32[2,1,64,128]{3,2,1,0:T(8,128)S(1)}, f32[2,1,64,128]{3,2,1,0:T(8,128)S(1)}, u32[]{:S(2)}, u32[]{:S(2)}) collective-permute-start(f32[2,1,64,128]{3,2,1,0:T(8,128)S(1)} %get-tuple-element.35), channel_id=1, source_target_pairs={{8,0},{16,8},{24,16},{32,24},{40,32},{48,40},{56,48},{64,56},{72,6... | collective-permute-start | bytes 196616 | tf_op jit(solution)/shard_map/ppermute | solution.py:30
  52.2 3.6 %collective-permute-done.9 = f32[2,1,64,128]{3,2,1,0:T(8,128)S(1)} collective-permute-done((f32[2,1,64,128]{3,2,1,0:T(8,128)S(1)}, f32[2,1,64,128]{3,2,1,0:T(8,128)S(1)}, u32[]{:S(2)}, u32[]{:S(2)}) %collective-permute-start.9) | collective-permute-done | bytes 65568 | tf_op jit(solution)/shard_map/ppermute | solution.py:30
  55.9 3.9 %collective-permute-start.10 = (f32[2,6,1,128]{3,2,1,0:T(1,128)S(1)}, f32[2,6,1,128]{3,2,1,0:T(1,128)S(1)}, u32[]{:S(2)}, u32[]{:S(2)}) collective-permute-start(f32[2,6,1,128]{3,2,1,0:T(1,128)S(1)} %get-tuple-element.28), channel_id=1, source_target_pairs={{0,1},{1,2},{2,3},{3,4},{4,5},{5,6},{6,7},{8,9},{9,10},{10,11},{11... | collective-permute-start | bytes 18440 | tf_op jit(solution)/shard_map/ppermute | solution.py:28
  59.8 1.3 collective-permute-start.11
  61.1 3.3 %collective-permute-done.11 = f32[2,6,1,128]{3,2,1,0:T(1,128)S(1)} collective-permute-done((f32[2,6,1,128]{3,2,1,0:T(1,128)S(1)}, f32[2,6,1,128]{3,2,1,0:T(1,128)S(1)}, u32[]{:S(2)}, u32[]{:S(2)}) %collective-permute-start.11) | collective-permute-done | bytes 6176 | tf_op jit(solution)/shard_map/ppermute | solution.py:30
  64.9 9.8 %reshape.77 = f32[2,2,32,2,64,2]{5,4,3,2,1,0:T(8,128)} reshape(f32[4,64,128]{2,1,0:T(8,128)S(1)} %fusion.25) | data formatting | bytes 262144 | tf_op jit(solution)/shard_map/reshape | solution.py:86
  74.7 4.0 %reduce_sum.49 = f32[2,32,64]{2,1,0:T(8,128)S(1)} reduce(f32[2,2,32,2,64,2]{5,4,3,2,1,0:T(8,128)} %reshape.77, f32[]{:T(128)} %constant.61.clone.1), dimensions={1,3,5}, to_apply=%region_1.2 | reduce | flops 28672 | bytes 147460 | tf_op jit(solution)/shard_map/reduce_sum | solution.py:86
  78.8 9.8 %reshape.78 = f32[2,2,32,2,64,2]{5,4,3,2,1,0:T(8,128)} reshape(f32[4,64,128]{2,1,0:T(8,128)S(1)} %get-tuple-element.39) | data formatting | bytes 262144 | tf_op jit(solution)/shard_map/reshape | solution.py:86
  88.6 4.0 %reduce_sum.50 = f32[2,32,64]{2,1,0:T(8,128)S(1)} reduce(f32[2,2,32,2,64,2]{5,4,3,2,1,0:T(8,128)} %reshape.78, f32[]{:T(128)} %constant.61.clone.1), dimensions={1,3,5}, to_apply=%region_2.3 | reduce | flops 28672 | bytes 147460 | tf_op jit(solution)/shard_map/reduce_sum | solution.py:86
  93.7 16.8 %all-to-all-start = ((f32[128,2,128]{2,1,0:T(2,128)}), f32[128,2,128]{2,1,0:T(2,128)S(1)}, u32[]{:S(2)}, u32[]{:S(2)}) async-start(f32[128,2,128]{2,1,0:T(2,128)} %copy.13), calls=%async_computation | async-start | bytes 262144 | tf_op jit(solution)/shard_map/all_to_all | solution.py:173
  111.8 10.9 %all-to-all-done = f32[128,2,128]{2,1,0:T(2,128)S(1)} async-done(((f32[128,2,128]{2,1,0:T(2,128)}), f32[128,2,128]{2,1,0:T(2,128)S(1)}, u32[]{:S(2)}, u32[]{:S(2)}) %all-to-all-start) | async-done | bytes 131104 | tf_op jit(solution)/shard_map/all_to_all | solution.py:173
  123.9 6.2 %all-to-all-start.1 = ((f32[128,2,128]{2,1,0:T(2,128)}), f32[128,2,128]{2,1,0:T(2,128)S(1)}, u32[]{:S(2)}, u32[]{:S(2)}) async-start(f32[128,2,128]{2,1,0:T(2,128)} %broadcast_in_dim.57), calls=%async_computation.1 | async-start | bytes 262144 | tf_op jit(solution)/shard_map/all_to_all | solution.py:176
  130.2 12.2 %all-to-all-done.1 = f32[128,2,128]{2,1,0:T(2,128)S(1)} async-done(((f32[128,2,128]{2,1,0:T(2,128)}), f32[128,2,128]{2,1,0:T(2,128)S(1)}, u32[]{:S(2)}, u32[]{:S(2)}) %all-to-all-start.1) | async-done | bytes 131104 | tf_op jit(solution)/shard_map/all_to_all | solution.py:176
  142.7 3.9 %broadcast_in_dim.59 = f32[2,2,32,2,64,2]{5,4,3,2,1,0:T(8,128)} broadcast(f32[2,32,64]{2,1,0:T(8,128)S(1)} %get-tuple-element.44), dimensions={0,2,4} | broadcast | bytes 147456 | tf_op jit(solution)/shard_map/broadcast_in_dim | solution.py:91
  146.6 6.9 %reshape.81 = f32[4,64,128]{2,1,0:T(8,128)S(1)} reshape(f32[2,2,32,2,64,2]{5,4,3,2,1,0:T(8,128)} %broadcast_in_dim.59) | data formatting | bytes 262144 | tf_op jit(solution)/shard_map/reshape | solution.py:92
  153.5 3.9 %broadcast_in_dim.58 = f32[2,2,32,2,64,2]{5,4,3,2,1,0:T(8,128)} broadcast(f32[2,32,64]{2,1,0:T(8,128)S(1)} %get-tuple-element.45), dimensions={0,2,4} | broadcast | bytes 147456 | tf_op jit(solution)/shard_map/broadcast_in_dim | solution.py:91
  157.4 6.9 %reshape.80 = f32[4,64,128]{2,1,0:T(8,128)S(1)} reshape(f32[2,2,32,2,64,2]{5,4,3,2,1,0:T(8,128)} %broadcast_in_dim.58) | data formatting | bytes 262144 | tf_op jit(solution)/shard_map/reshape | solution.py:92
  164.3 3.1 %collective-permute-start.12 = (f32[2,1,64,128]{3,2,1,0:T(8,128)S(1)}, f32[2,1,64,128]{3,2,1,0:T(8,128)S(1)}, u32[]{:S(2)}, u32[]{:S(2)}) collective-permute-start(f32[2,1,64,128]{3,2,1,0:T(8,128)S(1)} %get-tuple-element.32), channel_id=1, source_target_pairs={{0,8},{8,16},{16,24},{24,32},{32,40},{40,48},{48,56},{56,64},{64,7... | collective-permute-start | bytes 196616 | tf_op jit(solution)/shard_map/ppermute | solution.py:28
  167.5 1.9 %collective-permute-start.13 = (f32[2,1,64,128]{3,2,1,0:T(8,128)S(1)}, f32[2,1,64,128]{3,2,1,0:T(8,128)S(1)}, u32[]{:S(2)}, u32[]{:S(2)}) collective-permute-start(f32[2,1,64,128]{3,2,1,0:T(8,128)S(1)} %get-tuple-element.33), channel_id=1, source_target_pairs={{8,0},{16,8},{24,16},{32,24},{40,32},{48,40},{56,48},{64,56},{72,6... | collective-permute-start | bytes 196616 | tf_op jit(solution)/shard_map/ppermute | solution.py:30
  169.4 3.6 %collective-permute-done.13 = f32[2,1,64,128]{3,2,1,0:T(8,128)S(1)} collective-permute-done((f32[2,1,64,128]{3,2,1,0:T(8,128)S(1)}, f32[2,1,64,128]{3,2,1,0:T(8,128)S(1)}, u32[]{:S(2)}, u32[]{:S(2)}) %collective-permute-start.13) | collective-permute-done | bytes 65568 | tf_op jit(solution)/shard_map/ppermute | solution.py:30
  173.1 4.8 %collective-permute-start.14 = (f32[2,6,1,128]{3,2,1,0:T(1,128)S(1)}, f32[2,6,1,128]{3,2,1,0:T(1,128)S(1)}, u32[]{:S(2)}, u32[]{:S(2)}) collective-permute-start(f32[2,6,1,128]{3,2,1,0:T(1,128)S(1)} %get-tuple-element.26), channel_id=1, source_target_pairs={{0,1},{1,2},{2,3},{3,4},{4,5},{5,6},{6,7},{8,9},{9,10},{10,11},{11... | collective-permute-start | bytes 18440 | tf_op jit(solution)/shard_map/ppermute | solution.py:28
  179.2 4.8 %collective-permute-done.15 = f32[2,6,1,128]{3,2,1,0:T(1,128)S(1)} collective-permute-done((f32[2,6,1,128]{3,2,1,0:T(1,128)S(1)}, f32[2,6,1,128]{3,2,1,0:T(1,128)S(1)}, u32[]{:S(2)}, u32[]{:S(2)}) %collective-permute-start.15) | collective-permute-done | bytes 6176 | tf_op jit(solution)/shard_map/ppermute | solution.py:30
  (71 shorter events, 15.6 us)
Async XLA Ops:
  0.6 64.1 %copy-start.1 = (f32[4,64,128]{2,1,0:T(8,128)S(1)}, f32[4,64,128]{2,1,0:T(8,128)}, u32[]{:S(2)}) copy-start(f32[4,64,128]{2,1,0:T(8,128)} %param.10) | copy-start | bytes 393220
  0.6 63.9 %copy-start = (f32[4,64,128]{2,1,0:T(8,128)S(1)}, f32[4,64,128]{2,1,0:T(8,128)}, u32[]{:S(2)}) copy-start(f32[4,64,128]{2,1,0:T(8,128)} %param.11) | copy-start | bytes 393220
  8.5 29.7 %collective-permute-start.4 = (f32[1,64,128]{2,1,0:T(8,128)S(1)}, f32[1,64,128]{2,1,0:T(8,128)S(1)}, u32[]{:S(2)}, u32[]{:S(2)}) collective-permute-start(f32[1,64,128]{2,1,0:T(8,128)S(1)} %get-tuple-element.43), channel_id=1, source_target_pairs={{8,0},{16,8},{24,16},{32,24},{40,32},{48,40},{56,48},{64,56},{72,6... | collective-permute-start | bytes 98312 | tf_op jit(solution)/shard_map/ppermute | solution.py:30
  24.6 13.7 %collective-permute-start.5 = (f32[1,64,128]{2,1,0:T(8,128)S(1)}, f32[1,64,128]{2,1,0:T(8,128)S(1)}, u32[]{:S(2)}, u32[]{:S(2)}) collective-permute-start(f32[1,64,128]{2,1,0:T(8,128)S(1)} %get-tuple-element.42), channel_id=1, source_target_pairs={{0,8},{8,16},{16,24},{24,32},{32,40},{40,48},{48,56},{56,64},{64,7... | collective-permute-start | bytes 98312 | tf_op jit(solution)/shard_map/ppermute | solution.py:28
  27.3 5.6 %collective-permute-start = (f32[2,1,64,128]{3,2,1,0:T(8,128)S(1)}, f32[2,1,64,128]{3,2,1,0:T(8,128)S(1)}, u32[]{:S(2)}, u32[]{:S(2)}) collective-permute-start(f32[2,1,64,128]{3,2,1,0:T(8,128)S(1)} %get-tuple-element.36), channel_id=1, source_target_pairs={{0,8},{8,16},{16,24},{24,32},{32,40},{40,48},{48,56},{56,64},{64,7... | collective-permute-start | bytes 196616 | tf_op jit(solution)/shard_map/ppermute | solution.py:28
  29.2 5.6 %collective-permute-start.1 = (f32[2,1,64,128]{3,2,1,0:T(8,128)S(1)}, f32[2,1,64,128]{3,2,1,0:T(8,128)S(1)}, u32[]{:S(2)}, u32[]{:S(2)}) collective-permute-start(f32[2,1,64,128]{3,2,1,0:T(8,128)S(1)} %get-tuple-element.37), channel_id=1, source_target_pairs={{8,0},{16,8},{24,16},{32,24},{40,32},{48,40},{56,48},{64,56},{72,6... | collective-permute-start | bytes 196616 | tf_op jit(solution)/shard_map/ppermute | solution.py:30
  35.6 8.6 %collective-permute-start.2 = (f32[2,6,1,128]{3,2,1,0:T(1,128)S(1)}, f32[2,6,1,128]{3,2,1,0:T(1,128)S(1)}, u32[]{:S(2)}, u32[]{:S(2)}) collective-permute-start(f32[2,6,1,128]{3,2,1,0:T(1,128)S(1)} %get-tuple-element.30), channel_id=1, source_target_pairs={{0,1},{1,2},{2,3},{3,4},{4,5},{5,6},{6,7},{8,9},{9,10},{10,11},{11... | collective-permute-start | bytes 18440 | tf_op jit(solution)/shard_map/ppermute | solution.py:28
  36.9 7.3 %collective-permute-start.3 = (f32[2,6,1,128]{3,2,1,0:T(1,128)S(1)}, f32[2,6,1,128]{3,2,1,0:T(1,128)S(1)}, u32[]{:S(2)}, u32[]{:S(2)}) collective-permute-start(f32[2,6,1,128]{3,2,1,0:T(1,128)S(1)} %get-tuple-element.31), channel_id=1, source_target_pairs={{1,0},{2,1},{3,2},{4,3},{5,4},{6,5},{7,6},{9,8},{10,9},{11,10},{12... | collective-permute-start | bytes 18440 | tf_op jit(solution)/shard_map/ppermute | solution.py:30
  38.2 7.0 %collective-permute-start.6 = (f32[6,1,128]{2,1,0:T(1,128)S(1)}, f32[6,1,128]{2,1,0:T(1,128)S(1)}, u32[]{:S(2)}, u32[]{:S(2)}) collective-permute-start(f32[6,1,128]{2,1,0:T(1,128)S(1)} %get-tuple-element.40), channel_id=1, source_target_pairs={{1,0},{2,1},{3,2},{4,3},{5,4},{6,5},{7,6},{9,8},{10,9},{11,10},{12... | collective-permute-start | bytes 9224 | tf_op jit(solution)/shard_map/ppermute | solution.py:30
  39.5 5.8 %collective-permute-start.7 = (f32[6,1,128]{2,1,0:T(1,128)S(1)}, f32[6,1,128]{2,1,0:T(1,128)S(1)}, u32[]{:S(2)}, u32[]{:S(2)}) collective-permute-start(f32[6,1,128]{2,1,0:T(1,128)S(1)} %get-tuple-element.41), channel_id=1, source_target_pairs={{0,1},{1,2},{2,3},{3,4},{4,5},{5,6},{6,7},{8,9},{9,10},{10,11},{11... | collective-permute-start | bytes 9224 | tf_op jit(solution)/shard_map/ppermute | solution.py:28
  47.7 4.5 %collective-permute-start.8 = (f32[2,1,64,128]{3,2,1,0:T(8,128)S(1)}, f32[2,1,64,128]{3,2,1,0:T(8,128)S(1)}, u32[]{:S(2)}, u32[]{:S(2)}) collective-permute-start(f32[2,1,64,128]{3,2,1,0:T(8,128)S(1)} %get-tuple-element.34), channel_id=1, source_target_pairs={{0,8},{8,16},{16,24},{24,32},{32,40},{40,48},{48,56},{56,64},{64,7... | collective-permute-start | bytes 196616 | tf_op jit(solution)/shard_map/ppermute | solution.py:28
  50.3 5.6 %collective-permute-start.9 = (f32[2,1,64,128]{3,2,1,0:T(8,128)S(1)}, f32[2,1,64,128]{3,2,1,0:T(8,128)S(1)}, u32[]{:S(2)}, u32[]{:S(2)}) collective-permute-start(f32[2,1,64,128]{3,2,1,0:T(8,128)S(1)} %get-tuple-element.35), channel_id=1, source_target_pairs={{8,0},{16,8},{24,16},{32,24},{40,32},{48,40},{56,48},{64,56},{72,6... | collective-permute-start | bytes 196616 | tf_op jit(solution)/shard_map/ppermute | solution.py:30
  55.9 5.2 %collective-permute-start.10 = (f32[2,6,1,128]{3,2,1,0:T(1,128)S(1)}, f32[2,6,1,128]{3,2,1,0:T(1,128)S(1)}, u32[]{:S(2)}, u32[]{:S(2)}) collective-permute-start(f32[2,6,1,128]{3,2,1,0:T(1,128)S(1)} %get-tuple-element.28), channel_id=1, source_target_pairs={{0,1},{1,2},{2,3},{3,4},{4,5},{5,6},{6,7},{8,9},{9,10},{10,11},{11... | collective-permute-start | bytes 18440 | tf_op jit(solution)/shard_map/ppermute | solution.py:28
  59.8 4.7 %collective-permute-start.11 = (f32[2,6,1,128]{3,2,1,0:T(1,128)S(1)}, f32[2,6,1,128]{3,2,1,0:T(1,128)S(1)}, u32[]{:S(2)}, u32[]{:S(2)}) collective-permute-start(f32[2,6,1,128]{3,2,1,0:T(1,128)S(1)} %get-tuple-element.29), channel_id=1, source_target_pairs={{1,0},{2,1},{3,2},{4,3},{5,4},{6,5},{7,6},{9,8},{10,9},{11,10},{12... | collective-permute-start | bytes 18440 | tf_op jit(solution)/shard_map/ppermute | solution.py:30
  78.8 31.8 %copy-start.2 = (s32[128,64]{0,1:T(8,128)S(1)}, s32[128,64]{0,1:T(8,128)}, u32[]{:S(2)}) copy-start(s32[128,64]{0,1:T(8,128)} %param.15) | copy-start | bytes 98308
  93.7 29.0 %all-to-all-start = ((f32[128,2,128]{2,1,0:T(2,128)}), f32[128,2,128]{2,1,0:T(2,128)S(1)}, u32[]{:S(2)}, u32[]{:S(2)}) async-start(f32[128,2,128]{2,1,0:T(2,128)} %copy.13), calls=%async_computation | async-start | bytes 262144 | tf_op jit(solution)/shard_map/all_to_all | solution.py:173
  123.9 18.5 %all-to-all-start.1 = ((f32[128,2,128]{2,1,0:T(2,128)}), f32[128,2,128]{2,1,0:T(2,128)S(1)}, u32[]{:S(2)}, u32[]{:S(2)}) async-start(f32[128,2,128]{2,1,0:T(2,128)} %broadcast_in_dim.57), calls=%async_computation.1 | async-start | bytes 262144 | tf_op jit(solution)/shard_map/all_to_all | solution.py:176
  164.3 5.1 %collective-permute-start.12 = (f32[2,1,64,128]{3,2,1,0:T(8,128)S(1)}, f32[2,1,64,128]{3,2,1,0:T(8,128)S(1)}, u32[]{:S(2)}, u32[]{:S(2)}) collective-permute-start(f32[2,1,64,128]{3,2,1,0:T(8,128)S(1)} %get-tuple-element.32), channel_id=1, source_target_pairs={{0,8},{8,16},{16,24},{24,32},{32,40},{40,48},{48,56},{56,64},{64,7... | collective-permute-start | bytes 196616 | tf_op jit(solution)/shard_map/ppermute | solution.py:28
  167.5 5.6 %collective-permute-start.13 = (f32[2,1,64,128]{3,2,1,0:T(8,128)S(1)}, f32[2,1,64,128]{3,2,1,0:T(8,128)S(1)}, u32[]{:S(2)}, u32[]{:S(2)}) collective-permute-start(f32[2,1,64,128]{3,2,1,0:T(8,128)S(1)} %get-tuple-element.33), channel_id=1, source_target_pairs={{8,0},{16,8},{24,16},{32,24},{40,32},{48,40},{56,48},{64,56},{72,6... | collective-permute-start | bytes 196616 | tf_op jit(solution)/shard_map/ppermute | solution.py:30
  173.1 6.2 %collective-permute-start.14 = (f32[2,6,1,128]{3,2,1,0:T(1,128)S(1)}, f32[2,6,1,128]{3,2,1,0:T(1,128)S(1)}, u32[]{:S(2)}, u32[]{:S(2)}) collective-permute-start(f32[2,6,1,128]{3,2,1,0:T(1,128)S(1)} %get-tuple-element.26), channel_id=1, source_target_pairs={{0,1},{1,2},{2,3},{3,4},{4,5},{5,6},{6,7},{8,9},{9,10},{10,11},{11... | collective-permute-start | bytes 18440 | tf_op jit(solution)/shard_map/ppermute | solution.py:28
  177.9 6.1 %collective-permute-start.15 = (f32[2,6,1,128]{3,2,1,0:T(1,128)S(1)}, f32[2,6,1,128]{3,2,1,0:T(1,128)S(1)}, u32[]{:S(2)}, u32[]{:S(2)}) collective-permute-start(f32[2,6,1,128]{3,2,1,0:T(1,128)S(1)} %get-tuple-element.27), channel_id=1, source_target_pairs={{1,0},{2,1},{3,2},{4,3},{5,4},{6,5},{7,6},{9,8},{10,9},{11,10},{12... | collective-permute-start | bytes 18440 | tf_op jit(solution)/shard_map/ppermute | solution.py:30
where the time goes:
time: 188 us; the launch traced here: 186 us
  starting transfers between devices  74.7 us (40%)
  local copies, waits for them, and re-layouts  45.4 us (24%)
  waiting for transfers between devices  40.5 us (22%)
  other arithmetic  22.6 us (12%)
    ppermute x8, starting transfers between devices, with_halo(): lax.ppermute(head, axis, [((i + 1) % count, i) for i in range(ends)])  27.5 us
    ppermute x8, starting transfers between devices, with_halo(): lax.ppermute(tail, axis, [(i, (i + 1) % count) for i in range(ends)])  24.2 us
    reshape x2, local copies, waits for them, and re-layouts, restrict(): field.reshape(size_x // 2, 2, size_y // 2, 2, size_p // 2, 2)  19.6 us
    ppermute x8, waiting for transfers between devices, with_halo(): lax.ppermute(head, axis, [((i + 1) % count, i) for i in range(ends)])  17.4 us
    all_to_all x1, starting transfers between devices, on_device(): lax.all_to_all(outgoing, 'gx', split_axis=0, concat_axis=0, tiled=True)  16.8 us
    reshape x2, local copies, waits for them, and re-layouts, prolong(): return wide.reshape(2 * size_x, 2 * size_y, 2 * size_p)  13.8 us
    all_to_all x1, waiting for transfers between devices, on_device(): lax.all_to_all(reply, 'gx', split_axis=0, concat_axis=0, tiled=True)  12.2 us
    all_to_all x1, waiting for transfers between devices, on_device(): lax.all_to_all(outgoing, 'gx', split_axis=0, concat_axis=0, tiled=True)  10.9 us
  transfers between devices with their start and end apart: 18, of which 7 were waited for; matrix products, arithmetic and copies ran while one was open for 2% of the time, Pallas kernels for 0%

commit v1 on v0

v1 whole, which is shorter than its diff:
```python
import functools

import jax
import jax.numpy as jnp
from jax import lax
from jax.experimental import pallas as pl
from jax.experimental.pallas import tpu as pltpu
from jax.sharding import PartitionSpec as P

NCLASS = 8
CSWEEP = 3
XROWS = 4
YCELLS = 64
PLANES = 128
PAD = 8
XGROUP = 8

relax_fine = 0.6
relax_coarse = 0.6
coarse_flux = 0.0625
coarse_bend = 0.125
coarse_det = 1.15625

F32 = jnp.float32
B16 = jnp.bfloat16
MESH = pl.DeviceIdType.MESH


def iota(shape, dim):
    return lax.broadcasted_iota(jnp.int32, shape, dim)


def halves(values):
    high = values.astype(B16)
    return high, (values - high.astype(F32)).astype(B16)


def dot(a, b):
    return jnp.dot(a, b, preferred_element_type=F32)


def dot_t(a, b):
    return lax.dot_general(a, b, (((1,), (1,)), ((), ())), preferred_element_type=F32)


def kernel(
    n_gx, n_gy,
    conc_h, pot_h, mass_h, psrc_h, mask_h, class_h, table, owner_h,
    conc_o, pot_o,
    fld, src, mask_v, class_v, owner_v,
    w_x, w_y, w_z, w_d, w_a, new,
    r_hi, r_mid, place, pick, edge_pick, count_v,
    totals, rs_buf, part, ar_buf, sol, y_out, y_in, corr,
    load_sem, ex_send, ex_recv, n_send, n_recv, g_send, g_recv, y_send, y_recv,
):
    ring = n_gx // XGROUP
    gx = lax.axis_index("gx")
    gy = lax.axis_index("gy")
    r = gx % ring
    q = gx // ring
    left, right = (gx + n_gx - 1) % n_gx, (gx + 1) % n_gx
    below, above = (gy + n_gy - 1) % n_gy, (gy + 1) % n_gy
    first, last = PAD, PAD + YCELLS

    def load(source, target, index):
        copy = pltpu.make_async_copy(source, target, load_sem.at[index])
        copy.start()
        return copy

    inner = pl.ds(PAD, YCELLS)
    l_mask = load(mask_h, mask_v, 0)
    l_class = load(class_h, class_v, 1)
    l_conc = load(conc_h, fld.at[0, pl.ds(1, XROWS), inner, :], 2)
    l_pot = load(pot_h, fld.at[1, pl.ds(1, XROWS), inner, :], 3)
    l_mass = load(mass_h, src.at[0, :, inner, :], 4)
    l_psrc = load(psrc_h, src.at[1, :, inner, :], 5)
    l_owner = load(owner_h, owner_v, 6)

    barrier = pltpu.get_barrier_semaphore()

    def greet(a, b):
        pl.semaphore_signal(barrier, inc=1, device_id=(a, b), device_id_type=MESH)

    for a in (left, right):
        greet(a, gy)
        for b in (below, above):
            greet(a, b)
    for b in (below, above):
        greet(gx, b)

    def greet_ring(i, carry):
        greet(q * ring + (r + 1 + i) % ring, gy)
        return carry

    def greet_group(i, carry):
        greet(((q + 1 + i) % XGROUP) * ring + r, gy)
        return carry

    lax.fori_loop(0, ring - 1, greet_ring, 0)
    lax.fori_loop(0, XGROUP - 1, greet_group, 0)

    l_mask.wait()
    l_class.wait()
    for x in range(XROWS):
        classes = class_v[x]
        values = jnp.zeros(classes.shape, F32)
        for marker in range(NCLASS):
            values = jnp.where(classes == marker, table[marker], values)
        fld[2, x + 1, inner, :] = mask_v[x].astype(F32) * values
    for copy in (l_conc, l_pot, l_mass, l_psrc, l_owner):
        copy.wait()
    pl.semaphore_wait(barrier, 8 + ring - 1 + XGROUP - 1)

    def remote(source, target, send, recv, device):
        copy = pltpu.make_async_remote_copy(
            src_ref=source, dst_ref=target, send_sem=send, recv_sem=recv, device_id=device, device_id_type=MESH
        )
        copy.start()
        return copy

    head, tail = pl.ds(first, PAD), pl.ds(last - PAD, PAD)
    over, under = pl.ds(last, PAD), pl.ds(0, PAD)
    rows = pl.ds(1, XROWS)
    plan = [
        (fld.at[:, 1, inner], fld.at[:, XROWS + 1, inner], (left, gy)),
        (fld.at[:, XROWS, inner], fld.at[:, 0, inner], (right, gy)),
        (fld.at[:, rows, head], fld.at[:, rows, over], (gx, below)),
        (fld.at[:, rows, tail], fld.at[:, rows, under], (gx, above)),
        (src.at[:, :, head], src.at[:, :, over], (gx, below)),
        (src.at[:, :, tail], src.at[:, :, under], (gx, above)),
        (fld.at[:, 1, head], fld.at[:, XROWS + 1, over], (left, below)),
        (fld.at[:, 1, tail], fld.at[:, XROWS + 1, under], (left, above)),
        (fld.at[:, XROWS, head], fld.at[:, 0, over], (right, below)),
        (fld.at[:, XROWS, tail], fld.at[:, 0, under], (right, above)),
    ]
    ex = [remote(a, b, ex_send.at[i], ex_recv.at[i], dev) for i, (a, b, dev) in enumerate(plan)]

    half = XROWS // 2
    lanes = half * YCELLS * 2
    half_y = YCELLS // 2
    n_cols = half * half_y

    def spread(rows_n, base):
        k = iota((rows_n, n_cols), 0) + base
        block = k // YCELLS
        column = jnp.where((block == 0) | (block == 2), half_y, 0) + (k % YCELLS) // 2
        return (iota((rows_n, n_cols), 1) == column).astype(F32).astype(B16)

    def owners(g):
        return owner_v[pl.ds(g, 1), :].astype(F32)

    own_p, own_m, own_n = owners(left), owners(gx), owners(right)
    off_l = jnp.where(gx == 0, 1, 0)
    off_r = jnp.where(gx == n_gx - 1, 1, 0)

    def wide(values, rows_n):
        return jnp.broadcast_to(values, (rows_n, n_cols)).astype(B16)

    all_rows = spread(lanes, 0)
    lane_block = iota((8, lanes), 1) // YCELLS
    row_p = dot_t(wide(own_p, 8), all_rows)
    row_m = dot_t(wide(own_m, 8), all_rows)
    row_n = dot_t(wide(own_n, 8), all_rows)
    lane_own = jnp.where(lane_block == 0, row_p - 1000.0 * off_l.astype(F32), row_m)
    lane_own = jnp.where(lane_block == 3, row_n - 1000.0 * off_r.astype(F32), lane_own)
    lane_own = lane_own[0:1, :].astype(jnp.int32)
    place[...] = jnp.where(iota((n_gx, lanes), 0) == lane_own, 0.125, 0.0).astype(B16)

    lane = iota((8, n_gx), 1)
    slot = lane // 8 + r + 1
    slot = jnp.where(slot >= ring, slot - ring, slot)
    lane_agg = (slot * 8 + lane % 8)[0:1, :].astype(F32)

    def picks(rows_n, base, values, off):
        column = dot_t(spread(rows_n, base), wide(values, n_gx)) - 1000.0 * off
        return (column == lane_agg).astype(F32).astype(B16)

    pick[0:YCELLS, :] = picks(YCELLS, 0, own_p, off_l.astype(F32))
    pick[YCELLS : 3 * YCELLS, :] = picks(2 * YCELLS, YCELLS, own_m, 0.0)
    pick[3 * YCELLS :, :] = picks(YCELLS, 3 * YCELLS, own_n, off_r.astype(F32))
    e_row = iota((16, n_cols), 0)
    e_col = jnp.where(e_row % 8 == 1, half_y, 0) + jnp.where(e_row >= 8, half_y - 1, 0)
    e_sel = (iota((16, n_cols), 1) == e_col).astype(F32).astype(B16)
    edge_pick[...] = (dot_t(e_sel, wide(own_m, n_gx)) == lane_agg).astype(F32).astype(B16)

    for copy in ex:
        copy.wait_recv()

    @pl.when(gx == 0)
    def _():
        for f in range(3):
            fld[f, 0] = jnp.zeros((YCELLS + 2 * PAD, PLANES), F32)

    @pl.when(gx == n_gx - 1)
    def _():
        for f in range(3):
            fld[f, XROWS + 1] = jnp.zeros((YCELLS + 2 * PAD, PLANES), F32)

    @pl.when(gy == 0)
    def _():
        for f in range(3):
            for x in range(XROWS + 2):
                fld[f, x, 0:PAD, :] = jnp.zeros((PAD, PLANES), F32)

    @pl.when(gy == n_gy - 1)
    def _():
        for f in range(3):
            for x in range(XROWS + 2):
                fld[f, x, last : last + PAD, :] = jnp.zeros((PAD, PLANES), F32)

    def edge_masks(rows_n):
        z = iota((rows_n, PLANES), 1)
        return z == 0, z == PLANES - 1

    def z_sum(value, low, high):
        return jnp.where(high, 0.0, pltpu.roll(value, PLANES - 1, 1)) + jnp.where(low, 0.0, pltpu.roll(value, 1, 1))

    def sweep_one(j, carry):
        base = 1 + 8 * j
        mid, up, dn = pl.ds(base, 8), pl.ds(base + 1, 8), pl.ds(base - 1, 8)
        low, high = edge_masks(8)
        mob = [fld[2, x, mid, :] for x in range(XROWS + 2)]
        face_x = [0.125 * (mob[x] + mob[x + 1]) for x in range(XROWS + 1)]
        for x in range(XROWS + 1):
            w_x[x, mid, :] = face_x[x]
        cc = [fld[0, x, mid, :] for x in range(XROWS + 2)]
        uu = [fld[1, x, mid, :] for x in range(XROWS + 2)]
        for x in range(1, XROWS + 1):
            m, c, u = mob[x], cc[x], uu[x]
            y_up = 0.125 * (m + fld[2, x, up, :])
            y_dn = 0.125 * (m + fld[2, x, dn, :])
            z_up = 0.125 * (m + jnp.where(high, 0.0, pltpu.roll(m, PLANES - 1, 1)))
            z_dn = jnp.where(low, 0.125 * m, pltpu.roll(z_up, 1, 1))
            diagonal = face_x[x - 1] + face_x[x] + y_up + y_dn + z_up + z_dn
            step = relax_fine / (1.0 + 4.0 * diagonal)
            z_w = jnp.where(high, 0.0, z_up)
            w_y[0, x - 1, mid, :] = y_dn
            w_y[1, x - 1, mid, :] = y_up
            w_z[x - 1, mid, :] = z_w
            w_d[x - 1, mid, :] = diagonal
            w_a[x - 1, mid, :] = step
            flow = face_x[x] * uu[x + 1] + face_x[x - 1] * uu[x - 1]
            flow = flow + y_up * fld[1, x, up, :] + y_dn * fld[1, x, dn, :]
            flow = flow + z_w * pltpu.roll(u, PLANES - 1, 1) + pltpu.roll(z_w * u, 1, 1)
            around = cc[x + 1] + cc[x - 1] + fld[0, x, up, :] + fld[0, x, dn, :] + z_sum(c, low, high)
            excess_mass = src[0, x - 1, mid, :] - c + flow - diagonal * u
            excess_pot = src[1, x - 1, mid, :] - u + 4.0 * c - 0.5 * around
            new[0, x, mid, :] = c + step * (excess_mass - diagonal * excess_pot)
            new[1, x, mid, :] = u + step * (excess_pot + 4.0 * excess_mass)
        return carry

    lax.fori_loop(0, (YCELLS + 8) // 8, sweep_one, 0)

    @pl.when(gy == 0)
    def _():
        for f in range(2):
            for x in range(1, XROWS + 1):
                new[f, x, 0:PAD, :] = jnp.zeros((PAD, PLANES), F32)

    @pl.when(gy == n_gy - 1)
    def _():
        for f in range(2):
            for x in range(1, XROWS + 1):
                new[f, x, last : last + PAD, :] = jnp.zeros((PAD, PLANES), F32)

    def excess(x, base, rows_n, low, high, cc, uu):
        mid, up, dn = pl.ds(base, rows_n), pl.ds(base + 1, rows_n), pl.ds(base - 1, rows_n)
        c, u = cc[x], uu[x]
        z_w, diagonal = w_z[x - 1, mid, :], w_d[x - 1, mid, :]
        flow = w_y[1, x - 1, mid, :] * new[1, x, up, :] + w_y[0, x - 1, mid, :] * new[1, x, dn, :]
        flow = flow + z_w * pltpu.roll(u, PLANES - 1, 1) + pltpu.roll(z_w * u, 1, 1)
        around = new[0, x, up, :] + new[0, x, dn, :] + z_sum(c, low, high)
        if (x + 1) in cc:
            flow = flow + w_x[x, mid, :] * uu[x + 1]
            around = around + cc[x + 1]
        if (x - 1) in cc:
            flow = flow + w_x[x - 1, mid, :] * uu[x - 1]
            around = around + cc[x - 1]
        excess_mass = src[0, x - 1, mid, :] - c + flow - diagonal * u
        excess_pot = src[1, x - 1, mid, :] - u + 4.0 * c - 0.5 * around
        return excess_mass, excess_pot, diagonal

    def collect(j, carry):
        base = pl.multiple_of(PAD + 16 * j, 8)
        mid = pl.ds(base, 16)
        low, high = edge_masks(16)
        cc = {x: new[0, x, mid, :] for x in range(1, XROWS + 1)}
        uu = {x: new[1, x, mid, :] for x in range(1, XROWS + 1)}
        got = [excess(x, base, 16, low, high, cc, uu) for x in range(1, XROWS + 1)]
        parts = [(w_x[0, mid, :] * uu[1], -0.5 * cc[1])]
        for i in range(half):
            parts.append((got[2 * i][0] + got[2 * i + 1][0], got[2 * i][1] + got[2 * i + 1][1]))
        parts.append((w_x[XROWS, mid, :] * uu[XROWS], -0.5 * cc[XROWS]))
        for block, pair in enumerate(parts):
            at = pl.ds(pl.multiple_of(block * YCELLS + 16 * j, 16), 16)
            for f in range(2):
                top, rest = halves(pair[f])
                r_hi[at, f * PLANES : (f + 1) * PLANES] = top
                r_mid[at, f * PLANES : (f + 1) * PLANES] = rest
        return carry

    lax.fori_loop(0, YCELLS // 16, collect, 0)

    fine = dot(place[...], r_hi[...]) + dot(place[...], r_mid[...])
    k = iota((2 * PLANES, PLANES), 0)
    pair_up = (iota((2 * PLANES, PLANES), 1) == (k // PLANES) * (PLANES // 2) + (k % PLANES) // 2).astype(F32).astype(B16)
    top, rest = halves(fine)
    totals[...] = (dot(top, pair_up) + dot(rest, pair_up)).reshape(ring, 8, PLANES)

    def scatter(i, carry):
        p = (r + 1 + i) % ring
        remote(totals.at[p], rs_buf.at[ring - 2 - i], g_send.at[0], g_recv.at[0], (q * ring + p, gy))
        return carry

    lax.fori_loop(0, ring - 1, scatter, 0)

    def all_of(ref, count, sem):
        pltpu.make_async_copy(ref.at[pl.ds(0, count)], ref.at[pl.ds(0, count)], sem).wait()

    tally = jnp.zeros((8, n_cols), F32)
    for j in range(8):
        hits = (owner_v[...] == r * 8 + j).astype(F32)
        tally = jnp.where(iota((8, n_cols), 0) == j, jnp.sum(hits, axis=0, keepdims=True), tally)
    count = dot(tally.astype(B16), jnp.ones((n_cols, PLANES), B16))
    count_v[...] = 1.0 / jnp.maximum(count, 1.0)

    all_of(rs_buf, ring - 1, g_recv.at[0])
    mine = totals[r]
    for i in range(ring - 1):
        mine = mine + rs_buf[i]
    part[...] = mine

    def swap(i, carry):
        p = (q + 1 + i) % XGROUP
        remote(part, ar_buf.at[XGROUP - 2 - i], g_send.at[1], g_recv.at[1], (p * ring + r, gy))
        return carry

    lax.fori_loop(0, XGROUP - 1, swap, 0)
    sides = [
        remote(new.at[:, 1, inner], new.at[:, XROWS + 1, inner], n_send.at[0], n_recv.at[0], (left, gy)),
        remote(new.at[:, XROWS, inner], new.at[:, 0, inner], n_send.at[1], n_recv.at[1], (right, gy)),
    ]
    all_of(ar_buf, XGROUP - 1, g_recv.at[1])
    for i in range(XGROUP - 1):
        mine = mine + ar_buf[i]
    mean = mine * count_v[...]

    hp = PLANES // 2
    z = iota((8, PLANES), 1)
    in_c = z < hp
    no_up = (z % hp) == hp - 1
    no_dn = (z % hp) == 0
    gap_pot = jnp.where(in_c, -2.0 * coarse_flux, 1.0 + 2.0 * coarse_bend)
    value = jnp.zeros((8, PLANES), F32)
    for step in range(CSWEEP):
        gap = mean
        if step:
            around = jnp.where(no_up, 0.0, pltpu.roll(value, PLANES - 1, 1)) + jnp.where(no_dn, 0.0, pltpu.roll(value, 1, 1))
            bend = 2.0 * value - around
            cross = jnp.where(in_c, value + coarse_bend * bend, coarse_flux * bend)
            moved = pltpu.roll(cross, hp, 1)
            gap = mean - value + jnp.where(in_c, -moved, moved)
        value = value + (relax_coarse / coarse_det) * (gap + gap_pot * pltpu.roll(gap, hp, 1))
    sol[ring - 1] = value
    part_out = sol.at[ring - 1]

    def gather(i, carry):
        p = (r + 1 + i) % ring
        remote(part_out, sol.at[ring - 2 - i], g_send.at[2], g_recv.at[2], (q * ring + p, gy))
        return carry

    lax.fori_loop(0, ring - 1, gather, 0)

    k = iota((2 * PLANES, 2 * PLANES), 0) % PLANES
    n = iota((2 * PLANES, 2 * PLANES), 1)
    widen = (k == (n // PLANES) * hp + (n % PLANES) // 2).astype(F32).astype(B16)

    all_of(sol, ring - 1, g_recv.at[2])
    solved = sol[...].reshape(n_gx, PLANES)
    both = jnp.concatenate(halves(solved), axis=1)

    edge = dot(edge_pick[...], both)
    edge = edge[:, :PLANES] + edge[:, PLANES:]
    y_out[...] = edge.reshape(2, 8, PLANES)
    ends = [
        remote(y_out.at[0], y_in.at[1], y_send.at[0], y_recv.at[0], (gx, below)),
        remote(y_out.at[1], y_in.at[0], y_send.at[1], y_recv.at[1], (gx, above)),
    ]
    corr[...] = dot(dot(pick[...], both).astype(B16), widen)

    for copy in sides:
        copy.wait()

    @pl.when(gx == 0)
    def _():
        for f in range(2):
            new[f, 0, inner, :] = jnp.zeros((YCELLS, PLANES), F32)

    @pl.when(gx == n_gx - 1)
    def _():
        for f in range(2):
            new[f, XROWS + 1, inner, :] = jnp.zeros((YCELLS, PLANES), F32)

    for x in range(XROWS + 2):
        block = (x + 1) // 2
        at = pl.ds(block * YCELLS, YCELLS)
        for f in range(2):
            new[f, x, inner, :] = new[f, x, inner, :] + corr[at, f * PLANES : (f + 1) * PLANES]

    for copy in ends:
        copy.wait()
    y_all = jnp.concatenate(halves(y_in[...].reshape(16, PLANES)), axis=1)
    y_fine = dot(y_all, widen)
    for side in range(2):
        row = PAD - 1 if side == 0 else last
        for x in range(1, XROWS + 1):
            for f in range(2):
                at = side * 8 + (x - 1) // 2
                add = y_fine[at : at + 1, f * PLANES : (f + 1) * PLANES]
                new[f, x, row : row + 1, :] = new[f, x, row : row + 1, :] + add

    @pl.when(gy == 0)
    def _():
        for f in range(2):
            for x in range(1, XROWS + 1):
                new[f, x, 0:PAD, :] = jnp.zeros((PAD, PLANES), F32)

    @pl.when(gy == n_gy - 1)
    def _():
        for f in range(2):
            for x in range(1, XROWS + 1):
                new[f, x, last : last + PAD, :] = jnp.zeros((PAD, PLANES), F32)

    def finish(j, carry):
        base = pl.multiple_of(PAD + 8 * j, 8)
        mid = pl.ds(base, 8)
        to = pl.ds(pl.multiple_of(8 * j, 8), 8)
        low, high = edge_masks(8)
        cc = {x: new[0, x, mid, :] for x in range(XROWS + 2)}
        uu = {x: new[1, x, mid, :] for x in range(XROWS + 2)}
        for x in range(1, XROWS + 1):
            excess_mass, excess_pot, diagonal = excess(x, base, 8, low, high, cc, uu)
            step = w_a[x - 1, mid, :]
            conc_o[x - 1, to, :] = cc[x] + step * (excess_mass - diagonal * excess_pot)
            pot_o[x - 1, to, :] = uu[x] + step * (excess_pot + 4.0 * excess_mass)
        return carry

    lax.fori_loop(0, YCELLS // 8, finish, 0)

    for copy in ex:
        copy.wait_send()
    all_of(rs_buf, ring - 1, g_send.at[0])
    all_of(ar_buf, XGROUP - 1, g_send.at[1])
    all_of(rs_buf, ring - 1, g_send.at[2])


def solution(mesh):
    n_gx, n_gy = mesh.shape["gx"], mesh.shape["gy"]
    ring = n_gx // XGROUP
    any_spec = pl.BlockSpec(memory_space=pl.ANY)
    y_pad = YCELLS + 2 * PAD
    k_all = 2 * XROWS // 2 * YCELLS

    def on_device(conc, pot, mass, psrc, mask, classes, table, owner):
        out = jax.ShapeDtypeStruct(conc.shape, F32)
        return pl.pallas_call(
            functools.partial(kernel, n_gx, n_gy),
            out_shape=(out, out),
            in_specs=[any_spec] * 6 + [pl.BlockSpec(memory_space=pltpu.SMEM), any_spec],
            out_specs=(pl.BlockSpec(memory_space=pltpu.VMEM),) * 2,
            scratch_shapes=[
                pltpu.VMEM((3, XROWS + 2, y_pad, PLANES), F32),
                pltpu.VMEM((2, XROWS, y_pad, PLANES), F32),
                pltpu.VMEM((XROWS, YCELLS, PLANES), jnp.int32),
                pltpu.VMEM((XROWS, YCELLS, PLANES), jnp.int32),
                pltpu.VMEM(owner.shape, jnp.int32),
                pltpu.VMEM((XROWS + 1, y_pad, PLANES), F32),
                pltpu.VMEM((2, XROWS, y_pad, PLANES), F32),
                pltpu.VMEM((XROWS, y_pad, PLANES), F32),
                pltpu.VMEM((XROWS, y_pad, PLANES), F32),
                pltpu.VMEM((XROWS, y_pad, PLANES), F32),
                pltpu.VMEM((2, XROWS + 2, y_pad, PLANES), F32),
                pltpu.VMEM((k_all, 2 * PLANES), B16),
                pltpu.VMEM((k_all, 2 * PLANES), B16),
                pltpu.VMEM((n_gx, k_all), B16),
                pltpu.VMEM((k_all, n_gx), B16),
                pltpu.VMEM((16, n_gx), B16),
                pltpu.VMEM((8, PLANES), F32),
                pltpu.VMEM((ring, 8, PLANES), F32),
                pltpu.VMEM((ring - 1, 8, PLANES), F32),
                pltpu.VMEM((8, PLANES), F32),
                pltpu.VMEM((XGROUP - 1, 8, PLANES), F32),
                pltpu.VMEM((ring, 8, PLANES), F32),
                pltpu.VMEM((2, 8, PLANES), F32),
                pltpu.VMEM((2, 8, PLANES), F32),
                pltpu.VMEM((k_all, 2 * PLANES), F32),
                pltpu.SemaphoreType.DMA((7,)),
                pltpu.SemaphoreType.DMA((10,)),
                pltpu.SemaphoreType.DMA((10,)),
                pltpu.SemaphoreType.DMA((2,)),
                pltpu.SemaphoreType.DMA((2,)),
                pltpu.SemaphoreType.DMA((3,)),
                pltpu.SemaphoreType.DMA((3,)),
                pltpu.SemaphoreType.DMA((2,)),
                pltpu.SemaphoreType.DMA((2,)),
            ],
            compiler_params=pltpu.CompilerParams(collective_id=0, has_side_effects=True, vmem_limit_bytes=60 << 20),
        )(conc, pot, mass, psrc, mask, classes, table, owner)

    field = P("gx", "gy", None)
    return jax.shard_map(
        on_device,
        mesh=mesh,
        in_specs=(field,) * 6 + (P(), P(None, "gy")),
        out_specs=(field, field),
        check_vma=False,
    )
```

time: 188 us -> 55 us (0.29)
  starting transfers between devices: 74.7 us -> 0 us
  Pallas kernels: 0 us -> 50.3 us
  local copies, waits for them, and re-layouts: 45.4 us -> 3.75 us
  waiting for transfers between devices: 40.5 us -> 0 us
  other arithmetic: 22.6 us -> 0 us
    ppermute x16 -> x0, starting transfers between devices: 51.7 us -> none  [the longest x8 27.5 us: with_halo(): lax.ppermute(head, axis, [((i + 1) % count, i) for i in range(ends)])]
    pallas_call x0 -> x1, Pallas kernels: none -> 50.3 us  [on_device(): pl.pallas_call(functools.partial(kernel, n_gx, n_gy), out_shape=(out, out...]
    reshape x4 -> x0, local copies, waits for them, and re-layouts: 33.4 us -> none  [the longest x2 19.6 us: restrict(): field.reshape(size_x // 2, 2, size_y // 2, 2, size_p // 2, 2)]
    all_to_all x2 -> x0, waiting for transfers between devices: 23.1 us -> none  [the longest x1 12.2 us: on_device(): lax.all_to_all(reply, 'gx', split_axis=0, concat_axis=0, tiled=True)]
    all_to_all x2 -> x0, starting transfers between devices: 23 us -> none  [the longest x1 16.8 us: on_device(): lax.all_to_all(outgoing, 'gx', split_axis=0, concat_axis=0, tiled=True)]
    ppermute x16 -> x0, waiting for transfers between devices: 17.4 us -> none  [the longest x8 17.4 us: with_halo(): lax.ppermute(head, axis, [((i + 1) % count, i) for i in range(ends)])]
    reduce_sum x4 -> x0, other arithmetic: 8.78 us -> none  [the longest x2 8.02 us: restrict(): field.reshape(size_x // 2, 2, size_y // 2, 2, size_p // 2, 2)]
    broadcast_in_dim x3 -> x0, local copies, waits for them, and re-layouts: 8.44 us -> none  [the longest x2 7.75 us: prolong(): jnp.broadcast_to(coarse[:, None, :, None, :, None], (size_x, 2, size_y, 2...]
  transfers between devices with their start and end apart: 18 -> 0, of which waited for: 7 -> 0; matrix products, arithmetic and copies ran while one was open for 2% -> 0% of each run, Pallas kernels for 0% -> 0%
where the time goes in v1:
time: 55 us; the launch traced here: 54.7 us
  Pallas kernels  50.3 us (91%)
  local copies, waits for them, and re-layouts  3.75 us (7%)
  between operations  0.65 us (1%)
    pallas_call x1, Pallas kernels, on_device(): pl.pallas_call(functools.partial(kernel, n_gx, n_gy), out_shape=(out, out...  50.3 us
    unnamed x5, local copies, waits for them, and re-layouts  3.75 us

profile of v1, /device:TPU:1, one launch (start us, length us, event | category | flops | bytes accessed | tf_op | source)
XLA Modules:
  0.0 54.7 jit_solution(2345893571479796561)
XLA Ops:
  0.6 1.5 %copy.10.owner_h = s32[128,64]{1,0:T(8,128)} copy(s32[128,64]{0,1:T(8,128)} %param.15) | data formatting | bytes 65536 | tf_op args[7]
  2.1 50.3 %shard_map.95 = (f32[4,64,128]{2,1,0:T(8,128)}, f32[4,64,128]{2,1,0:T(8,128)}) custom-call(f32[4,64,128]{2,1,0:T(8,128)} %conc_h.1, f32[4,64,128]{2,1,0:T(8,128)} %pot_h.1, f32[4,64,128]{2,1,0:T(8,128)} %mass_h.1, f32[4,64,128]{2,1,0:T(8,128)} %psrc_h.1, s32[4,64,128]{2,1,0:T(8,128)} %mask_h.1, s32[4,64,128]{2,1,0:T(8,128)} %class_h.1, f32[8]{0:T(128)} %table.1, ...), custom_call_target="tpu_custom_call" | custom-call | tf_op jit(solution)/shard_map/pallas_call | solution.py:466
  52.5 0.0 copy-start
  52.5 1.6 %copy.13 = f32[4,64,128]{2,1,0:T(8,128)} copy(f32[4,64,128]{2,1,0:T(8,128)} %get-tuple-element.4) | data formatting | bytes 262144
  54.1 0.0 copy-done
  54.1 0.7 %copy.14 = f32[4,64,128]{2,1,0:T(8,128)} copy(f32[4,64,128]{2,1,0:T(8,128)S(1)} %copy-done) | data formatting | bytes 262144
Async XLA Ops:
  52.5 1.6 %copy-start = (f32[4,64,128]{2,1,0:T(8,128)S(1)}, f32[4,64,128]{2,1,0:T(8,128)}, u32[]{:S(2)}) copy-start(f32[4,64,128]{2,1,0:T(8,128)} %get-tuple-element.5) | copy-start | bytes 393220

commit v2 on v1

--- a/solution.py
+++ b/solution.py
@@ -45,9 +45,9 @@
 
 def kernel(
     n_gx, n_gy,
-    conc_h, pot_h, mass_h, psrc_h, mask_h, class_h, table, owner_h,
+    conc_h, pot_h, mass_h, psrc_h, mask_h, class_h, table_h, owner_h,
     conc_o, pot_o,
-    fld, src, mask_v, class_v, owner_v,
+    fld, src, mask_v, class_v, owner_v, table,
     w_x, w_y, w_z, w_d, w_a, new,
     r_hi, r_mid, place, pick, edge_pick, count_v,
     totals, rs_buf, part, ar_buf, sol, y_out, y_in, corr,
@@ -62,43 +62,55 @@
     below, above = (gy + n_gy - 1) % n_gy, (gy + 1) % n_gy
     first, last = PAD, PAD + YCELLS
 
+    chips = ring // 2
+    y_chip, core = r // 2, r % 2
+
+    def away(i, count):
+        return count // 2 + ((i + 1) // 2) * (1 - 2 * (i % 2))
+
+    def ring_at(offset, cross):
+        return ((y_chip + offset) % chips) * 2 + (1 - core if cross else core)
+
+    barrier = pltpu.get_barrier_semaphore()
+
+    def greet(a, b):
+        pl.semaphore_signal(barrier, inc=1, device_id=(a, b), device_id_type=MESH)
+
+    def greet_ring(i, carry):
+        for cross in range(2):
+            greet(q * ring + ring_at(away(i, chips), cross), gy)
+        return carry
+
+    def greet_group(i, carry):
+        greet(((q + away(i, XGROUP)) % XGROUP) * ring + r, gy)
+        return carry
+
+    lax.fori_loop(0, XGROUP - 1, greet_group, 0)
+    lax.fori_loop(0, chips - 1, greet_ring, 0)
+    for a in (left, right):
+        for b in (below, above):
+            greet(a, b)
+        greet(a, gy)
+    for b in (below, above):
+        greet(gx, b)
+    greet(q * ring + ring_at(0, 1), gy)
+
     def load(source, target, index):
         copy = pltpu.make_async_copy(source, target, load_sem.at[index])
         copy.start()
         return copy
 
     inner = pl.ds(PAD, YCELLS)
+    l_table = load(table_h, table, 7)
+    l_class = load(class_h, class_v, 1)
     l_mask = load(mask_h, mask_v, 0)
-    l_class = load(class_h, class_v, 1)
     l_conc = load(conc_h, fld.at[0, pl.ds(1, XROWS), inner, :], 2)
     l_pot = load(pot_h, fld.at[1, pl.ds(1, XROWS), inner, :], 3)
     l_mass = load(mass_h, src.at[0, :, inner, :], 4)
     l_psrc = load(psrc_h, src.at[1, :, inner, :], 5)
     l_owner = load(owner_h, owner_v, 6)
 
-    barrier = pltpu.get_barrier_semaphore()
-
-    def greet(a, b):
-        pl.semaphore_signal(barrier, inc=1, device_id=(a, b), device_id_type=MESH)
-
-    for a in (left, right):
-        greet(a, gy)
-        for b in (below, above):
-            greet(a, b)
-    for b in (below, above):
-        greet(gx, b)
-
-    def greet_ring(i, carry):
-        greet(q * ring + (r + 1 + i) % ring, gy)
-        return carry
-
-    def greet_group(i, carry):
-        greet(((q + 1 + i) % XGROUP) * ring + r, gy)
-        return carry
-
-    lax.fori_loop(0, ring - 1, greet_ring, 0)
-    lax.fori_loop(0, XGROUP - 1, greet_group, 0)
-
+    l_table.wait()
     l_mask.wait()
     l_class.wait()
     for x in range(XROWS):
@@ -118,20 +130,22 @@
         copy.start()
         return copy
 
-    head, tail = pl.ds(first, PAD), pl.ds(last - PAD, PAD)
-    over, under = pl.ds(last, PAD), pl.ds(0, PAD)
+    head, tail = pl.ds(first, 2), pl.ds(last - 2, 2)
+    over, under = pl.ds(last, 2), pl.ds(first - 2, 2)
+    head_1, tail_1 = pl.ds(first, 1), pl.ds(last - 1, 1)
+    over_1, under_1 = pl.ds(last, 1), pl.ds(first - 1, 1)
     rows = pl.ds(1, XROWS)
     plan = [
         (fld.at[:, 1, inner], fld.at[:, XROWS + 1, inner], (left, gy)),
         (fld.at[:, XROWS, inner], fld.at[:, 0, inner], (right, gy)),
         (fld.at[:, rows, head], fld.at[:, rows, over], (gx, below)),
         (fld.at[:, rows, tail], fld.at[:, rows, under], (gx, above)),
-        (src.at[:, :, head], src.at[:, :, over], (gx, below)),
-        (src.at[:, :, tail], src.at[:, :, under], (gx, above)),
-        (fld.at[:, 1, head], fld.at[:, XROWS + 1, over], (left, below)),
-        (fld.at[:, 1, tail], fld.at[:, XROWS + 1, under], (left, above)),
-        (fld.at[:, XROWS, head], fld.at[:, 0, over], (right, below)),
-        (fld.at[:, XROWS, tail], fld.at[:, 0, under], (right, above)),
+        (src.at[:, :, head_1], src.at[:, :, over_1], (gx, below)),
+        (src.at[:, :, tail_1], src.at[:, :, under_1], (gx, above)),
+        (fld.at[:, 1, head_1], fld.at[:, XROWS + 1, over_1], (left, below)),
+        (fld.at[:, 1, tail_1], fld.at[:, XROWS + 1, under_1], (left, above)),
+        (fld.at[:, XROWS, head_1], fld.at[:, 0, over_1], (right, below)),
+        (fld.at[:, XROWS, tail_1], fld.at[:, 0, under_1], (right, above)),
     ]
     ex = [remote(a, b, ex_send.at[i], ex_recv.at[i], dev) for i, (a, b, dev) in enumerate(plan)]
 
@@ -146,10 +160,11 @@
         column = jnp.where((block == 0) | (block == 2), half_y, 0) + (k % YCELLS) // 2
         return (iota((rows_n, n_cols), 1) == column).astype(F32).astype(B16)
 
-    def owners(g):
-        return owner_v[pl.ds(g, 1), :].astype(F32)
-
-    own_p, own_m, own_n = owners(left), owners(gx), owners(right)
+    which = iota((8, n_gx), 0)
+    chosen = jnp.where(which == 0, left, jnp.where(which == 1, gx, right))
+    one_hot = (iota((8, n_gx), 1) == chosen).astype(F32).astype(B16)
+    three = dot_t(one_hot, owner_v[...].astype(F32).astype(B16))
+    own_p, own_m, own_n = three[0:1, :], three[1:2, :], three[2:3, :]
     off_l = jnp.where(gx == 0, 1, 0)
     off_r = jnp.where(gx == n_gx - 1, 1, 0)
 
@@ -167,9 +182,11 @@
     place[...] = jnp.where(iota((n_gx, lanes), 0) == lane_own, 0.125, 0.0).astype(B16)
 
     lane = iota((8, n_gx), 1)
-    slot = lane // 8 + r + 1
-    slot = jnp.where(slot >= ring, slot - ring, slot)
-    lane_agg = (slot * 8 + lane % 8)[0:1, :].astype(F32)
+    origin = jnp.where(lane // 8 == ring - 1, r, ring_at(0, 1))
+    for k in range(chips - 1):
+        for cross in range(2):
+            origin = jnp.where(lane // 8 == 2 * k + cross, ring_at(chips - away(k, chips), cross), origin)
+    lane_agg = (origin * 8 + lane % 8)[0:1, :].astype(F32)
 
     def picks(rows_n, base, values, off):
         column = dot_t(spread(rows_n, base), wide(values, n_gx)) - 1000.0 * off
@@ -183,31 +200,6 @@
     e_sel = (iota((16, n_cols), 1) == e_col).astype(F32).astype(B16)
     edge_pick[...] = (dot_t(e_sel, wide(own_m, n_gx)) == lane_agg).astype(F32).astype(B16)
 
-    for copy in ex:
-        copy.wait_recv()
-
-    @pl.when(gx == 0)
-    def _():
-        for f in range(3):
-            fld[f, 0] = jnp.zeros((YCELLS + 2 * PAD, PLANES), F32)
-
-    @pl.when(gx == n_gx - 1)
-    def _():
-        for f in range(3):
-            fld[f, XROWS + 1] = jnp.zeros((YCELLS + 2 * PAD, PLANES), F32)
-
-    @pl.when(gy == 0)
-    def _():
-        for f in range(3):
-            for x in range(XROWS + 2):
-                fld[f, x, 0:PAD, :] = jnp.zeros((PAD, PLANES), F32)
-
-    @pl.when(gy == n_gy - 1)
-    def _():
-        for f in range(3):
-            for x in range(XROWS + 2):
-                fld[f, x, last : last + PAD, :] = jnp.zeros((PAD, PLANES), F32)
-
     def edge_masks(rows_n):
         z = iota((rows_n, PLANES), 1)
         return z == 0, z == PLANES - 1
@@ -215,17 +207,18 @@
     def z_sum(value, low, high):
         return jnp.where(high, 0.0, pltpu.roll(value, PLANES - 1, 1)) + jnp.where(low, 0.0, pltpu.roll(value, 1, 1))
 
-    def sweep_one(j, carry):
-        base = 1 + 8 * j
+    def sweep(base, chosen):
         mid, up, dn = pl.ds(base, 8), pl.ds(base + 1, 8), pl.ds(base - 1, 8)
         low, high = edge_masks(8)
-        mob = [fld[2, x, mid, :] for x in range(XROWS + 2)]
-        face_x = [0.125 * (mob[x] + mob[x + 1]) for x in range(XROWS + 1)]
-        for x in range(XROWS + 1):
-            w_x[x, mid, :] = face_x[x]
-        cc = [fld[0, x, mid, :] for x in range(XROWS + 2)]
-        uu = [fld[1, x, mid, :] for x in range(XROWS + 2)]
-        for x in range(1, XROWS + 1):
+        need = sorted({x + d for x in chosen for d in (-1, 0, 1)})
+        mob = {x: fld[2, x, mid, :] for x in need}
+        cc = {x: fld[0, x, mid, :] for x in need}
+        uu = {x: fld[1, x, mid, :] for x in need}
+        face_x = {x: 0.125 * (mob[x] + mob[x + 1]) for x in need if x + 1 in mob}
+        for x in chosen:
+            w_x[x - 1, mid, :] = face_x[x - 1]
+            if x + 1 not in chosen:
+                w_x[x, mid, :] = face_x[x]
             m, c, u = mob[x], cc[x], uu[x]
             y_up = 0.125 * (m + fld[2, x, up, :])
             y_dn = 0.125 * (m + fld[2, x, dn, :])
@@ -247,9 +240,45 @@
             excess_pot = src[1, x - 1, mid, :] - u + 4.0 * c - 0.5 * around
             new[0, x, mid, :] = c + step * (excess_mass - diagonal * excess_pot)
             new[1, x, mid, :] = u + step * (excess_pot + 4.0 * excess_mass)
-        return carry
-
-    lax.fori_loop(0, (YCELLS + 8) // 8, sweep_one, 0)
+
+    def sweeps(count, base, stride, chosen):
+        def body(j, carry):
+            sweep(base + stride * j, chosen)
+            return carry
+
+        lax.fori_loop(0, count, body, 0)
+
+    middle = tuple(range(2, XROWS))
+    sweeps((YCELLS - 8) // 8, first + 1, 8, middle)
+    sweeps(1, last - 9, 8, middle)
+
+    for copy in ex:
+        copy.wait_recv()
+
+    @pl.when(gx == 0)
+    def _():
+        for f in range(3):
+            fld[f, 0] = jnp.zeros((YCELLS + 2 * PAD, PLANES), F32)
+
+    @pl.when(gx == n_gx - 1)
+    def _():
+        for f in range(3):
+            fld[f, XROWS + 1] = jnp.zeros((YCELLS + 2 * PAD, PLANES), F32)
+
+    @pl.when(gy == 0)
+    def _():
+        for f in range(3):
+            for x in range(XROWS + 2):
+                fld[f, x, 0:PAD, :] = jnp.zeros((PAD, PLANES), F32)
+
+    @pl.when(gy == n_gy - 1)
+    def _():
+        for f in range(3):
+            for x in range(XROWS + 2):
+                fld[f, x, last : last + PAD, :] = jnp.zeros((PAD, PLANES), F32)
+
+    sweeps((YCELLS + 8) // 8, 1, 8, (1, XROWS))
+    sweeps(2, 1, YCELLS, middle)
 
     @pl.when(gy == 0)
     def _():
@@ -307,21 +336,29 @@
     top, rest = halves(fine)
     totals[...] = (dot(top, pair_up) + dot(rest, pair_up)).reshape(ring, 8, PLANES)
 
-    def scatter(i, carry):
-        p = (r + 1 + i) % ring
-        remote(totals.at[p], rs_buf.at[ring - 2 - i], g_send.at[0], g_recv.at[0], (q * ring + p, gy))
-        return carry
-
-    lax.fori_loop(0, ring - 1, scatter, 0)
+    def to_ring(source, target, index):
+        def one(offset, cross, slot):
+            p = ring_at(offset, cross)
+            remote(source(p), target.at[slot], g_send.at[index], g_recv.at[index], (q * ring + p, gy))
+
+        def body(i, carry):
+            for cross in range(2):
+                one(away(i, chips), cross, 2 * i + cross)
+            return carry
+
+        lax.fori_loop(0, chips - 1, body, 0)
+        one(0, 1, ring - 2)
+
+    to_ring(lambda p: totals.at[p], rs_buf, 0)
 
     def all_of(ref, count, sem):
         pltpu.make_async_copy(ref.at[pl.ds(0, count)], ref.at[pl.ds(0, count)], sem).wait()
 
-    tally = jnp.zeros((8, n_cols), F32)
+    tally = jnp.zeros((8, n_gx), F32)
     for j in range(8):
         hits = (owner_v[...] == r * 8 + j).astype(F32)
-        tally = jnp.where(iota((8, n_cols), 0) == j, jnp.sum(hits, axis=0, keepdims=True), tally)
-    count = dot(tally.astype(B16), jnp.ones((n_cols, PLANES), B16))
+        tally = jnp.where(iota((8, n_gx), 0) == j, jnp.sum(hits, axis=0, keepdims=True), tally)
+    count = dot(tally.astype(B16), jnp.ones((n_gx, PLANES), B16))
     count_v[...] = 1.0 / jnp.maximum(count, 1.0)
 
     all_of(rs_buf, ring - 1, g_recv.at[0])
@@ -331,8 +368,8 @@
     part[...] = mine
 
     def swap(i, carry):
-        p = (q + 1 + i) % XGROUP
-        remote(part, ar_buf.at[XGROUP - 2 - i], g_send.at[1], g_recv.at[1], (p * ring + r, gy))
+        p = (q + away(i, XGROUP)) % XGROUP
+        remote(part, ar_buf.at[i], g_send.at[1], g_recv.at[1], (p * ring + r, gy))
         return carry
 
     lax.fori_loop(0, XGROUP - 1, swap, 0)
@@ -362,14 +399,7 @@
             gap = mean - value + jnp.where(in_c, -moved, moved)
         value = value + (relax_coarse / coarse_det) * (gap + gap_pot * pltpu.roll(gap, hp, 1))
     sol[ring - 1] = value
-    part_out = sol.at[ring - 1]
-
-    def gather(i, carry):
-        p = (r + 1 + i) % ring
-        remote(part_out, sol.at[ring - 2 - i], g_send.at[2], g_recv.at[2], (q * ring + p, gy))
-        return carry
-
-    lax.fori_loop(0, ring - 1, gather, 0)
+    to_ring(lambda p: sol.at[ring - 1], sol, 2)
 
     k = iota((2 * PLANES, 2 * PLANES), 0) % PLANES
     n = iota((2 * PLANES, 2 * PLANES), 1)
@@ -406,30 +436,6 @@
         at = pl.ds(block * YCELLS, YCELLS)
         for f in range(2):
             new[f, x, inner, :] = new[f, x, inner, :] + corr[at, f * PLANES : (f + 1) * PLANES]
-
-    for copy in ends:
-        copy.wait()
-    y_all = jnp.concatenate(halves(y_in[...].reshape(16, PLANES)), axis=1)
-    y_fine = dot(y_all, widen)
-    for side in range(2):
-        row = PAD - 1 if side == 0 else last
-        for x in range(1, XROWS + 1):
-            for f in range(2):
-                at = side * 8 + (x - 1) // 2
-                add = y_fine[at : at + 1, f * PLANES : (f + 1) * PLANES]
-                new[f, x, row : row + 1, :] = new[f, x, row : row + 1, :] + add
-
-    @pl.when(gy == 0)
-    def _():
-        for f in range(2):
-            for x in range(1, XROWS + 1):
-                new[f, x, 0:PAD, :] = jnp.zeros((PAD, PLANES), F32)
-
-    @pl.when(gy == n_gy - 1)
-    def _():
-        for f in range(2):
-            for x in range(1, XROWS + 1):
-                new[f, x, last : last + PAD, :] = jnp.zeros((PAD, PLANES), F32)
 
     def finish(j, carry):
         base = pl.multiple_of(PAD + 8 * j, 8)
@@ -445,13 +451,53 @@
             pot_o[x - 1, to, :] = uu[x] + step * (excess_pot + 4.0 * excess_mass)
         return carry
 
-    lax.fori_loop(0, YCELLS // 8, finish, 0)
+    lax.fori_loop(1, YCELLS // 8 - 1, finish, 0)
+
+    for copy in ends:
+        copy.wait()
+    y_all = jnp.concatenate(halves(y_in[...].reshape(16, PLANES)), axis=1)
+    y_fine = dot(y_all, widen)
+    for side in range(2):
+        row = PAD - 1 if side == 0 else last
+        for x in range(1, XROWS + 1):
+            for f in range(2):
+                at = side * 8 + (x - 1) // 2
+                add = y_fine[at : at + 1, f * PLANES : (f + 1) * PLANES]
+                new[f, x, row : row + 1, :] = new[f, x, row : row + 1, :] + add
+
+    @pl.when(gy == 0)
+    def _():
+        for f in range(2):
+            for x in range(1, XROWS + 1):
+                new[f, x, 0:PAD, :] = jnp.zeros((PAD, PLANES), F32)
+
+    @pl.when(gy == n_gy - 1)
+    def _():
+        for f in range(2):
+            for x in range(1, XROWS + 1):
+                new[f, x, last : last + PAD, :] = jnp.zeros((PAD, PLANES), F32)
+
+    def finish_ends(j, carry):
+        return finish(j * (YCELLS // 8 - 1), carry)
+
+    lax.fori_loop(0, 2, finish_ends, 0)
 
     for copy in ex:
         copy.wait_send()
     all_of(rs_buf, ring - 1, g_send.at[0])
     all_of(ar_buf, XGROUP - 1, g_send.at[1])
     all_of(rs_buf, ring - 1, g_send.at[2])
+
+
+def hand_out(conc_v, pot_v, conc_o, pot_o, sem):
+    copies = [
+        pltpu.make_async_copy(conc_v, conc_o, sem.at[0]),
+        pltpu.make_async_copy(pot_v, pot_o, sem.at[1]),
+    ]
+    for copy in copies:
+        copy.start()
+    for copy in copies:
+        copy.wait()
 
 
 def solution(mesh):
@@ -463,17 +509,18 @@
 
     def on_device(conc, pot, mass, psrc, mask, classes, table, owner):
         out = jax.ShapeDtypeStruct(conc.shape, F32)
-        return pl.pallas_call(
+        held = pl.pallas_call(
             functools.partial(kernel, n_gx, n_gy),
             out_shape=(out, out),
-            in_specs=[any_spec] * 6 + [pl.BlockSpec(memory_space=pltpu.SMEM), any_spec],
+            in_specs=[any_spec] * 8,
             out_specs=(pl.BlockSpec(memory_space=pltpu.VMEM),) * 2,
             scratch_shapes=[
                 pltpu.VMEM((3, XROWS + 2, y_pad, PLANES), F32),
                 pltpu.VMEM((2, XROWS, y_pad, PLANES), F32),
                 pltpu.VMEM((XROWS, YCELLS, PLANES), jnp.int32),
                 pltpu.VMEM((XROWS, YCELLS, PLANES), jnp.int32),
-                pltpu.VMEM(owner.shape, jnp.int32),
+                pltpu.VMEM((owner.shape[1], owner.shape[0]), jnp.int32),
+                pltpu.SMEM((NCLASS,), F32),
                 pltpu.VMEM((XROWS + 1, y_pad, PLANES), F32),
                 pltpu.VMEM((2, XROWS, y_pad, PLANES), F32),
                 pltpu.VMEM((XROWS, y_pad, PLANES), F32),
@@ -494,7 +541,7 @@
                 pltpu.VMEM((2, 8, PLANES), F32),
                 pltpu.VMEM((2, 8, PLANES), F32),
                 pltpu.VMEM((k_all, 2 * PLANES), F32),
-                pltpu.SemaphoreType.DMA((7,)),
+                pltpu.SemaphoreType.DMA((8,)),
                 pltpu.SemaphoreType.DMA((10,)),
                 pltpu.SemaphoreType.DMA((10,)),
                 pltpu.SemaphoreType.DMA((2,)),
@@ -504,8 +551,16 @@
                 pltpu.SemaphoreType.DMA((2,)),
                 pltpu.SemaphoreType.DMA((2,)),
             ],
-            compiler_params=pltpu.CompilerParams(collective_id=0, has_side_effects=True, vmem_limit_bytes=60 << 20),
-        )(conc, pot, mass, psrc, mask, classes, table, owner)
+            compiler_params=pltpu.CompilerParams(collective_id=0, has_side_effects=True, vmem_limit_bytes=54912 << 10),
+        )(conc, pot, mass, psrc, mask, classes, table, owner.T)
+        return pl.pallas_call(
+            hand_out,
+            out_shape=(out, out),
+            in_specs=[pl.BlockSpec(memory_space=pltpu.VMEM)] * 2,
+            out_specs=(any_spec, any_spec),
+            scratch_shapes=[pltpu.SemaphoreType.DMA((2,))],
+            compiler_params=pltpu.CompilerParams(vmem_limit_bytes=1 << 20),
+        )(*held)
 
     field = P("gx", "gy", None)
     return jax.shard_map(

time: 55 us -> 51.1 us (0.929)
  local copies, waits for them, and re-layouts: 3.75 us -> 1.41 us
  Pallas kernels: 50.3 us -> 48.8 us
    unnamed x5 -> x4, local copies, waits for them, and re-layouts: 3.75 us -> 1.41 us
    pallas_call x1, Pallas kernels: 50.3 us -> 48.1 us  [on_device(): pl.pallas_call(functools.partial(kernel, n_gx, n_gy), out_shape=(out, out...]
    pallas_call x0 -> x1, Pallas kernels: none -> 0.72 us  [on_device(): pl.pallas_call(hand_out, out_shape=(out, out), in_specs=[pl.BlockSpec(mem...]
where the time goes in v2:
time: 51.1 us; the launch traced here: 50.9 us
  Pallas kernels  48.8 us (95%)
  local copies, waits for them, and re-layouts  1.41 us (3%)
  between operations  0.65 us (1%)
    pallas_call x1, Pallas kernels, on_device(): pl.pallas_call(functools.partial(kernel, n_gx, n_gy), out_shape=(out, out...  48.1 us
    unnamed x4, local copies, waits for them, and re-layouts  1.41 us

profile of v2, /device:TPU:1, one launch (start us, length us, event | category | flops | bytes accessed | tf_op | source)
XLA Modules:
  0.0 50.9 jit_solution(14547965228683107493)
XLA Ops:
  0.6 0.0 copy-start.1
  0.6 0.6 %copy-done.1 = f32[8]{0:T(128)S(1)} copy-done((f32[8]{0:T(128)S(1)}, f32[8]{0:T(128)}, u32[]{:S(2)}) %copy-start.1) | copy-done | bytes 56
  1.3 0.0 copy-start
  1.3 0.8 %copy-done = s32[128,64]{0,1:T(8,128)S(1)} copy-done((s32[128,64]{0,1:T(8,128)S(1)}, s32[128,64]{0,1:T(8,128)}, u32[]{:S(2)}) %copy-start) | copy-done | bytes 32792
  2.0 48.1 %shard_map.95 = (f32[4,64,128]{2,1,0:T(8,128)S(1)}, f32[4,64,128]{2,1,0:T(8,128)S(1)}) custom-call(f32[4,64,128]{2,1,0:T(8,128)} %conc_h.1, f32[4,64,128]{2,1,0:T(8,128)} %pot_h.1, f32[4,64,128]{2,1,0:T(8,128)} %mass_h.1, f32[4,64,128]{2,1,0:T(8,128)} %psrc_h.1, s32[4,64,128]{2,1,0:T(8,128)} %mask_h.1, s32[4,64,128]{2,1,0:T(8,128)} %class_h.1, ...), custom_call_target="tpu_custom_call" | custom-call | tf_op jit(solution)/shard_map/pallas_call | solution.py:512
  50.2 0.7 %shard_map.96 = (f32[4,64,128]{2,1,0:T(8,128)}, f32[4,64,128]{2,1,0:T(8,128)}) custom-call(f32[4,64,128]{2,1,0:T(8,128)S(1)} %get-tuple-element.4.conc_v, f32[4,64,128]{2,1,0:T(8,128)S(1)} %get-tuple-element.5.pot_v), custom_call_target="tpu_custom_call" | custom-call | tf_op jit(solution)/shard_map/pallas_call | solution.py:556
Async XLA Ops:
  0.6 0.7 %copy-start.1 = (f32[8]{0:T(128)S(1)}, f32[8]{0:T(128)}, u32[]{:S(2)}) copy-start(f32[8]{0:T(128)} %table_h.1) | copy-start | bytes 100
  1.3 0.8 %copy-start = (s32[128,64]{0,1:T(8,128)S(1)}, s32[128,64]{0,1:T(8,128)}, u32[]{:S(2)}) copy-start(s32[128,64]{0,1:T(8,128)} %param.15) | copy-start | bytes 98308

commit v3 on v2

--- a/solution.py
+++ b/solution.py
@@ -136,16 +136,16 @@
     over_1, under_1 = pl.ds(last, 1), pl.ds(first - 1, 1)
     rows = pl.ds(1, XROWS)
     plan = [
+        (fld.at[:, 1, head_1], fld.at[:, XROWS + 1, over_1], (left, below)),
+        (fld.at[:, 1, tail_1], fld.at[:, XROWS + 1, under_1], (left, above)),
+        (fld.at[:, XROWS, head_1], fld.at[:, 0, over_1], (right, below)),
+        (fld.at[:, XROWS, tail_1], fld.at[:, 0, under_1], (right, above)),
         (fld.at[:, 1, inner], fld.at[:, XROWS + 1, inner], (left, gy)),
         (fld.at[:, XROWS, inner], fld.at[:, 0, inner], (right, gy)),
         (fld.at[:, rows, head], fld.at[:, rows, over], (gx, below)),
         (fld.at[:, rows, tail], fld.at[:, rows, under], (gx, above)),
         (src.at[:, :, head_1], src.at[:, :, over_1], (gx, below)),
         (src.at[:, :, tail_1], src.at[:, :, under_1], (gx, above)),
-        (fld.at[:, 1, head_1], fld.at[:, XROWS + 1, over_1], (left, below)),
-        (fld.at[:, 1, tail_1], fld.at[:, XROWS + 1, under_1], (left, above)),
-        (fld.at[:, XROWS, head_1], fld.at[:, 0, over_1], (right, below)),
-        (fld.at[:, XROWS, tail_1], fld.at[:, 0, under_1], (right, above)),
     ]
     ex = [remote(a, b, ex_send.at[i], ex_recv.at[i], dev) for i, (a, b, dev) in enumerate(plan)]
 
@@ -207,50 +207,71 @@
     def z_sum(value, low, high):
         return jnp.where(high, 0.0, pltpu.roll(value, PLANES - 1, 1)) + jnp.where(low, 0.0, pltpu.roll(value, 1, 1))
 
-    def sweep(base, chosen):
+    def settle(x, mid, c, u, diagonal, mass_part, pot_part):
+        step = relax_fine / (1.0 + 4.0 * diagonal)
+        w_d[x - 1, mid, :] = diagonal
+        w_a[x - 1, mid, :] = step
+        excess_mass = mass_part - diagonal * u
+        new[0, x, mid, :] = c + step * (excess_mass - diagonal * pot_part)
+        new[1, x, mid, :] = u + step * (pot_part + 4.0 * excess_mass)
+
+    def sweep(base, with_sides):
         mid, up, dn = pl.ds(base, 8), pl.ds(base + 1, 8), pl.ds(base - 1, 8)
         low, high = edge_masks(8)
-        need = sorted({x + d for x in chosen for d in (-1, 0, 1)})
+        need = range(XROWS + 2) if with_sides else range(1, XROWS + 1)
         mob = {x: fld[2, x, mid, :] for x in need}
         cc = {x: fld[0, x, mid, :] for x in need}
         uu = {x: fld[1, x, mid, :] for x in need}
         face_x = {x: 0.125 * (mob[x] + mob[x + 1]) for x in need if x + 1 in mob}
-        for x in chosen:
-            w_x[x - 1, mid, :] = face_x[x - 1]
-            if x + 1 not in chosen:
-                w_x[x, mid, :] = face_x[x]
+        for x, face in face_x.items():
+            w_x[x, mid, :] = face
+        for x in range(1, XROWS + 1):
             m, c, u = mob[x], cc[x], uu[x]
             y_up = 0.125 * (m + fld[2, x, up, :])
             y_dn = 0.125 * (m + fld[2, x, dn, :])
             z_up = 0.125 * (m + jnp.where(high, 0.0, pltpu.roll(m, PLANES - 1, 1)))
             z_dn = jnp.where(low, 0.125 * m, pltpu.roll(z_up, 1, 1))
-            diagonal = face_x[x - 1] + face_x[x] + y_up + y_dn + z_up + z_dn
-            step = relax_fine / (1.0 + 4.0 * diagonal)
             z_w = jnp.where(high, 0.0, z_up)
             w_y[0, x - 1, mid, :] = y_dn
             w_y[1, x - 1, mid, :] = y_up
             w_z[x - 1, mid, :] = z_w
-            w_d[x - 1, mid, :] = diagonal
-            w_a[x - 1, mid, :] = step
-            flow = face_x[x] * uu[x + 1] + face_x[x - 1] * uu[x - 1]
-            flow = flow + y_up * fld[1, x, up, :] + y_dn * fld[1, x, dn, :]
-            flow = flow + z_w * pltpu.roll(u, PLANES - 1, 1) + pltpu.roll(z_w * u, 1, 1)
-            around = cc[x + 1] + cc[x - 1] + fld[0, x, up, :] + fld[0, x, dn, :] + z_sum(c, low, high)
-            excess_mass = src[0, x - 1, mid, :] - c + flow - diagonal * u
-            excess_pot = src[1, x - 1, mid, :] - u + 4.0 * c - 0.5 * around
-            new[0, x, mid, :] = c + step * (excess_mass - diagonal * excess_pot)
-            new[1, x, mid, :] = u + step * (excess_pot + 4.0 * excess_mass)
-
-    def sweeps(count, base, stride, chosen):
+            diagonal = (y_up + y_dn) + (z_up + z_dn)
+            flow = y_up * fld[1, x, up, :] + y_dn * fld[1, x, dn, :]
+            flow = flow + (z_w * pltpu.roll(u, PLANES - 1, 1) + pltpu.roll(z_w * u, 1, 1))
+            around = (fld[0, x, up, :] + fld[0, x, dn, :]) + z_sum(c, low, high)
+            for face, other in ((x, x + 1), (x - 1, x - 1)):
+                if face in face_x:
+                    diagonal = diagonal + face_x[face]
+                    flow = flow + face_x[face] * uu[other]
+                    around = around + cc[other]
+            mass_part = (src[0, x - 1, mid, :] - c) + flow
+            pot_part = (src[1, x - 1, mid, :] - u + 4.0 * c) - 0.5 * around
+            if x in face_x and x - 1 in face_x:
+                settle(x, mid, c, u, diagonal, mass_part, pot_part)
+            else:
+                w_d[x - 1, mid, :] = diagonal
+                new[0, x, mid, :] = mass_part
+                new[1, x, mid, :] = pot_part
+
+    def add_sides(base):
+        mid = pl.ds(base, 8)
+        for x, face, other in ((1, 0, 0), (XROWS, XROWS, XROWS + 1)):
+            weight = 0.125 * (fld[2, x, mid, :] + fld[2, other, mid, :])
+            w_x[face, mid, :] = weight
+            diagonal = w_d[x - 1, mid, :] + weight
+            mass_part = new[0, x, mid, :] + weight * fld[1, other, mid, :]
+            pot_part = new[1, x, mid, :] - 0.5 * fld[0, other, mid, :]
+            settle(x, mid, fld[0, x, mid, :], fld[1, x, mid, :], diagonal, mass_part, pot_part)
+
+    def over_rows(count, base, stride, do):
         def body(j, carry):
-            sweep(base + stride * j, chosen)
+            do(base + stride * j)
             return carry
 
         lax.fori_loop(0, count, body, 0)
 
-    middle = tuple(range(2, XROWS))
-    sweeps((YCELLS - 8) // 8, first + 1, 8, middle)
-    sweeps(1, last - 9, 8, middle)
+    n_mid = (YCELLS - 8) // 8
+    over_rows(n_mid, first + 1, 8, lambda base: sweep(base, False))
 
     for copy in ex:
         copy.wait_recv()
@@ -277,8 +298,8 @@
             for x in range(XROWS + 2):
                 fld[f, x, last : last + PAD, :] = jnp.zeros((PAD, PLANES), F32)
 
-    sweeps((YCELLS + 8) // 8, 1, 8, (1, XROWS))
-    sweeps(2, 1, YCELLS, middle)
+    over_rows(n_mid, first + 1, 8, add_sides)
+    over_rows(2, 1, YCELLS, lambda base: sweep(base, True))
 
     @pl.when(gy == 0)
     def _():
@@ -292,22 +313,16 @@
             for x in range(1, XROWS + 1):
                 new[f, x, last : last + PAD, :] = jnp.zeros((PAD, PLANES), F32)
 
-    def excess(x, base, rows_n, low, high, cc, uu):
+    def mass_excess(x, base, rows_n, cc, uu):
         mid, up, dn = pl.ds(base, rows_n), pl.ds(base + 1, rows_n), pl.ds(base - 1, rows_n)
-        c, u = cc[x], uu[x]
-        z_w, diagonal = w_z[x - 1, mid, :], w_d[x - 1, mid, :]
+        u, z_w = uu[x], w_z[x - 1, mid, :]
         flow = w_y[1, x - 1, mid, :] * new[1, x, up, :] + w_y[0, x - 1, mid, :] * new[1, x, dn, :]
-        flow = flow + z_w * pltpu.roll(u, PLANES - 1, 1) + pltpu.roll(z_w * u, 1, 1)
-        around = new[0, x, up, :] + new[0, x, dn, :] + z_sum(c, low, high)
-        if (x + 1) in cc:
+        flow = flow + (z_w * pltpu.roll(u, PLANES - 1, 1) + pltpu.roll(z_w * u, 1, 1))
+        if (x + 1) in uu:
             flow = flow + w_x[x, mid, :] * uu[x + 1]
-            around = around + cc[x + 1]
-        if (x - 1) in cc:
+        if (x - 1) in uu:
             flow = flow + w_x[x - 1, mid, :] * uu[x - 1]
-            around = around + cc[x - 1]
-        excess_mass = src[0, x - 1, mid, :] - c + flow - diagonal * u
-        excess_pot = src[1, x - 1, mid, :] - u + 4.0 * c - 0.5 * around
-        return excess_mass, excess_pot, diagonal
+        return (src[0, x - 1, mid, :] - cc[x]) + (flow - w_d[x - 1, mid, :] * u)
 
     def collect(j, carry):
         base = pl.multiple_of(PAD + 16 * j, 8)
@@ -315,10 +330,18 @@
         low, high = edge_masks(16)
         cc = {x: new[0, x, mid, :] for x in range(1, XROWS + 1)}
         uu = {x: new[1, x, mid, :] for x in range(1, XROWS + 1)}
-        got = [excess(x, base, 16, low, high, cc, uu) for x in range(1, XROWS + 1)]
+        mass = {x: mass_excess(x, base, 16, cc, uu) for x in cc}
+        up, dn = pl.ds(base + 1, 16), pl.ds(base - 1, 16)
         parts = [(w_x[0, mid, :] * uu[1], -0.5 * cc[1])]
-        for i in range(half):
-            parts.append((got[2 * i][0] + got[2 * i + 1][0], got[2 * i][1] + got[2 * i + 1][1]))
+        for a in range(1, XROWS, 2):
+            conc = cc[a] + cc[a + 1]
+            around = (new[0, a, up, :] + new[0, a + 1, up, :]) + (new[0, a, dn, :] + new[0, a + 1, dn, :])
+            around = around + z_sum(conc, low, high)
+            for other in (a - 1, a + 2):
+                if other in cc:
+                    around = around + cc[other]
+            psrc = src[1, a - 1, mid, :] + src[1, a, mid, :]
+            parts.append((mass[a] + mass[a + 1], psrc - (uu[a] + uu[a + 1]) + 3.5 * conc - 0.5 * around))
         parts.append((w_x[XROWS, mid, :] * uu[XROWS], -0.5 * cc[XROWS]))
         for block, pair in enumerate(parts):
             at = pl.ds(pl.multiple_of(block * YCELLS + 16 * j, 16), 16)
@@ -445,42 +468,33 @@
         cc = {x: new[0, x, mid, :] for x in range(XROWS + 2)}
         uu = {x: new[1, x, mid, :] for x in range(XROWS + 2)}
         for x in range(1, XROWS + 1):
-            excess_mass, excess_pot, diagonal = excess(x, base, 8, low, high, cc, uu)
-            step = w_a[x - 1, mid, :]
+            around = cc[x + 1] + cc[x - 1] + new[0, x, pl.ds(base + 1, 8), :] + new[0, x, pl.ds(base - 1, 8), :]
+            around = around + z_sum(cc[x], low, high)
+            excess_mass = mass_excess(x, base, 8, cc, uu)
+            excess_pot = src[1, x - 1, mid, :] - uu[x] + 4.0 * cc[x] - 0.5 * around
+            step, diagonal = w_a[x - 1, mid, :], w_d[x - 1, mid, :]
             conc_o[x - 1, to, :] = cc[x] + step * (excess_mass - diagonal * excess_pot)
             pot_o[x - 1, to, :] = uu[x] + step * (excess_pot + 4.0 * excess_mass)
         return carry
 
-    lax.fori_loop(1, YCELLS // 8 - 1, finish, 0)
+    lax.fori_loop(0, YCELLS // 8, finish, 0)
 
     for copy in ends:
         copy.wait()
-    y_all = jnp.concatenate(halves(y_in[...].reshape(16, PLANES)), axis=1)
-    y_fine = dot(y_all, widen)
+    y_fine = dot(jnp.concatenate(halves(y_in[...].reshape(16, PLANES)), axis=1), widen)
+    inside = (jnp.where(gy == 0, 0.0, 1.0), jnp.where(gy == n_gy - 1, 0.0, 1.0))
     for side in range(2):
-        row = PAD - 1 if side == 0 else last
-        for x in range(1, XROWS + 1):
-            for f in range(2):
-                at = side * 8 + (x - 1) // 2
-                add = y_fine[at : at + 1, f * PLANES : (f + 1) * PLANES]
-                new[f, x, row : row + 1, :] = new[f, x, row : row + 1, :] + add
-
-    @pl.when(gy == 0)
-    def _():
-        for f in range(2):
-            for x in range(1, XROWS + 1):
-                new[f, x, 0:PAD, :] = jnp.zeros((PAD, PLANES), F32)
-
-    @pl.when(gy == n_gy - 1)
-    def _():
-        for f in range(2):
-            for x in range(1, XROWS + 1):
-                new[f, x, last : last + PAD, :] = jnp.zeros((PAD, PLANES), F32)
-
-    def finish_ends(j, carry):
-        return finish(j * (YCELLS // 8 - 1), carry)
-
-    lax.fori_loop(0, 2, finish_ends, 0)
+        row, out_row = (first, 0) if side == 0 else (last - 1, YCELLS - 1)
+        for x in range(XROWS):
+            at = side * 8 + x // 2
+            add_conc = y_fine[at : at + 1, :PLANES] * inside[side]
+            add_pot = y_fine[at : at + 1, PLANES:] * inside[side]
+            step = w_a[x, row : row + 1, :]
+            mass = w_y[side, x, row : row + 1, :] * add_pot
+            pot = -0.5 * add_conc
+            spot = slice(out_row, out_row + 1)
+            conc_o[x, spot, :] = conc_o[x, spot, :] + step * (mass - w_d[x, row : row + 1, :] * pot)
+            pot_o[x, spot, :] = pot_o[x, spot, :] + step * (pot + 4.0 * mass)
 
     for copy in ex:
         copy.wait_send()
@@ -551,8 +565,8 @@
                 pltpu.SemaphoreType.DMA((2,)),
                 pltpu.SemaphoreType.DMA((2,)),
             ],
-            compiler_params=pltpu.CompilerParams(collective_id=0, has_side_effects=True, vmem_limit_bytes=54912 << 10),
-        )(conc, pot, mass, psrc, mask, classes, table, owner.T)
+            compiler_params=pltpu.CompilerParams(collective_id=0, has_side_effects=True, vmem_limit_bytes=24 << 20),
+        )(*(pltpu.with_memory_space_constraint(a, pltpu.HBM) for a in (conc, pot, mass, psrc, mask, classes, table, owner.T)))
         return pl.pallas_call(
             hand_out,
             out_shape=(out, out),

time: 51.1 us -> 47.8 us (0.935)
  Pallas kernels: 48.8 us -> 46.9 us
  local copies, waits for them, and re-layouts: 1.41 us -> 0 us
    pallas_call x1, Pallas kernels: 48.1 us -> 46.2 us  [on_device(): pl.pallas_call(functools.partial(kernel, n_gx, n_gy), out_shape=(out, out...]
    unnamed x4 -> x0, local copies, waits for them, and re-layouts: 1.41 us -> none
where the time goes in v3:
time: 47.8 us; the launch traced here: 47.6 us
  Pallas kernels  46.9 us (98%)
  between operations  0.64 us (1%)
    pallas_call x1, Pallas kernels, on_device(): pl.pallas_call(functools.partial(kernel, n_gx, n_gy), out_shape=(out, out...  46.2 us

profile of v3, /device:TPU:1, one launch (start us, length us, event | category | flops | bytes accessed | tf_op | source)
XLA Modules:
  0.0 47.6 jit_solution(6750470146733458359)
XLA Ops:
  0.6 46.2 %shard_map.95 = (f32[4,64,128]{2,1,0:T(8,128)S(1)}, f32[4,64,128]{2,1,0:T(8,128)S(1)}) custom-call(f32[4,64,128]{2,1,0:T(8,128)} %conc_h.1, f32[4,64,128]{2,1,0:T(8,128)} %pot_h.1, f32[4,64,128]{2,1,0:T(8,128)} %mass_h.1, f32[4,64,128]{2,1,0:T(8,128)} %psrc_h.1, s32[4,64,128]{2,1,0:T(8,128)} %mask_h.1, s32[4,64,128]{2,1,0:T(8,128)} %class_h.1, f32[8]{0:T(128)} %table_h.1, ...), custom_call_target="tpu_custom_call" | custom-call | tf_op jit(solution)/shard_map/pallas_call | solution.py:526
  46.9 0.7 %shard_map.96 = (f32[4,64,128]{2,1,0:T(8,128)}, f32[4,64,128]{2,1,0:T(8,128)}) custom-call(f32[4,64,128]{2,1,0:T(8,128)S(1)} %get-tuple-element.4.conc_v, f32[4,64,128]{2,1,0:T(8,128)S(1)} %get-tuple-element.5.pot_v), custom_call_target="tpu_custom_call" | custom-call | tf_op jit(solution)/shard_map/pallas_call | solution.py:570

commit v4 on v3

--- a/solution.py
+++ b/solution.py
@@ -50,7 +50,7 @@
     fld, src, mask_v, class_v, owner_v, table,
     w_x, w_y, w_z, w_d, w_a, new,
     r_hi, r_mid, place, pick, edge_pick, count_v,
-    totals, rs_buf, part, ar_buf, sol, y_out, y_in, corr,
+    totals, mate_buf, mixed, rs_buf, part, ar_buf, sol, y_out, y_in, corr,
     load_sem, ex_send, ex_recv, n_send, n_recv, g_send, g_recv, y_send, y_recv,
 ):
     ring = n_gx // XGROUP
@@ -68,32 +68,33 @@
     def away(i, count):
         return count // 2 + ((i + 1) // 2) * (1 - 2 * (i % 2))
 
-    def ring_at(offset, cross):
-        return ((y_chip + offset) % chips) * 2 + (1 - core if cross else core)
+    def ring_at(offset):
+        return ((y_chip + offset) % chips) * 2 + core
 
     barrier = pltpu.get_barrier_semaphore()
 
     def greet(a, b):
         pl.semaphore_signal(barrier, inc=1, device_id=(a, b), device_id_type=MESH)
 
+    def greet_far(i, carry):
+        greet(((q + away(i, XGROUP)) % XGROUP) * ring + r, gy)
+        if chips == XGROUP:
+            greet(q * ring + ring_at(away(i, chips)), gy)
+        return carry
+
     def greet_ring(i, carry):
-        for cross in range(2):
-            greet(q * ring + ring_at(away(i, chips), cross), gy)
+        greet(q * ring + ring_at(away(i, chips)), gy)
         return carry
 
-    def greet_group(i, carry):
-        greet(((q + away(i, XGROUP)) % XGROUP) * ring + r, gy)
-        return carry
-
-    lax.fori_loop(0, XGROUP - 1, greet_group, 0)
-    lax.fori_loop(0, chips - 1, greet_ring, 0)
+    lax.fori_loop(0, XGROUP - 1, greet_far, 0)
+    if chips != XGROUP:
+        lax.fori_loop(0, chips - 1, greet_ring, 0)
     for a in (left, right):
         for b in (below, above):
             greet(a, b)
         greet(a, gy)
     for b in (below, above):
         greet(gx, b)
-    greet(q * ring + ring_at(0, 1), gy)
 
     def load(source, target, index):
         copy = pltpu.make_async_copy(source, target, load_sem.at[index])
@@ -121,7 +122,7 @@
         fld[2, x + 1, inner, :] = mask_v[x].astype(F32) * values
     for copy in (l_conc, l_pot, l_mass, l_psrc, l_owner):
         copy.wait()
-    pl.semaphore_wait(barrier, 8 + ring - 1 + XGROUP - 1)
+    pl.semaphore_wait(barrier, 8 + chips - 1 + XGROUP - 1)
 
     def remote(source, target, send, recv, device):
         copy = pltpu.make_async_remote_copy(
@@ -135,13 +136,15 @@
     head_1, tail_1 = pl.ds(first, 1), pl.ds(last - 1, 1)
     over_1, under_1 = pl.ds(last, 1), pl.ds(first - 1, 1)
     rows = pl.ds(1, XROWS)
+    out_row, out_far, out_dev = 1 + (XROWS - 1) * core, (XROWS + 1) * (1 - core), (gx + n_gx + 2 * core - 1) % n_gx
+    in_row, in_far, in_dev = XROWS - (XROWS - 1) * core, (XROWS + 1) * core, (gx + n_gx + 1 - 2 * core) % n_gx
     plan = [
         (fld.at[:, 1, head_1], fld.at[:, XROWS + 1, over_1], (left, below)),
         (fld.at[:, 1, tail_1], fld.at[:, XROWS + 1, under_1], (left, above)),
         (fld.at[:, XROWS, head_1], fld.at[:, 0, over_1], (right, below)),
         (fld.at[:, XROWS, tail_1], fld.at[:, 0, under_1], (right, above)),
-        (fld.at[:, 1, inner], fld.at[:, XROWS + 1, inner], (left, gy)),
-        (fld.at[:, XROWS, inner], fld.at[:, 0, inner], (right, gy)),
+        (fld.at[:, out_row, inner], fld.at[:, out_far, inner], (out_dev, gy)),
+        (fld.at[:, in_row, inner], fld.at[:, in_far, inner], (in_dev, gy)),
         (fld.at[:, rows, head], fld.at[:, rows, over], (gx, below)),
         (fld.at[:, rows, tail], fld.at[:, rows, under], (gx, above)),
         (src.at[:, :, head_1], src.at[:, :, over_1], (gx, below)),
@@ -182,10 +185,11 @@
     place[...] = jnp.where(iota((n_gx, lanes), 0) == lane_own, 0.125, 0.0).astype(B16)
 
     lane = iota((8, n_gx), 1)
-    origin = jnp.where(lane // 8 == ring - 1, r, ring_at(0, 1))
+    at = (lane // 8) % chips
+    origin = jnp.where(at == chips - 1, r, 0)
     for k in range(chips - 1):
-        for cross in range(2):
-            origin = jnp.where(lane // 8 == 2 * k + cross, ring_at(chips - away(k, chips), cross), origin)
+        origin = jnp.where(at == k, ring_at(chips - away(k, chips)), origin)
+    origin = jnp.where(lane // 8 >= chips, origin + 1 - 2 * core, origin)
     lane_agg = (origin * 8 + lane % 8)[0:1, :].astype(F32)
 
     def picks(rows_n, base, values, off):
@@ -357,25 +361,25 @@
     k = iota((2 * PLANES, PLANES), 0)
     pair_up = (iota((2 * PLANES, PLANES), 1) == (k // PLANES) * (PLANES // 2) + (k % PLANES) // 2).astype(F32).astype(B16)
     top, rest = halves(fine)
-    totals[...] = (dot(top, pair_up) + dot(rest, pair_up)).reshape(ring, 8, PLANES)
+    totals[...] = (dot(top, pair_up) + dot(rest, pair_up)).reshape(chips, 2, 8, PLANES)
 
     def to_ring(source, target, index):
-        def one(offset, cross, slot):
-            p = ring_at(offset, cross)
-            remote(source(p), target.at[slot], g_send.at[index], g_recv.at[index], (q * ring + p, gy))
-
         def body(i, carry):
-            for cross in range(2):
-                one(away(i, chips), cross, 2 * i + cross)
+            p = (y_chip + away(i, chips)) % chips
+            remote(source(p), target.at[i], g_send.at[index], g_recv.at[index], (q * ring + p * 2 + core, gy))
             return carry
 
         lax.fori_loop(0, chips - 1, body, 0)
-        one(0, 1, ring - 2)
-
-    to_ring(lambda p: totals.at[p], rs_buf, 0)
 
     def all_of(ref, count, sem):
-        pltpu.make_async_copy(ref.at[pl.ds(0, count)], ref.at[pl.ds(0, count)], sem).wait()
+        if count:
+            pltpu.make_async_copy(ref.at[pl.ds(0, count)], ref.at[pl.ds(0, count)], sem).wait()
+
+    mate = (in_dev, gy)
+    swap_0 = remote(totals.at[:, 1 - core], mate_buf, g_send.at[0], g_recv.at[0], mate)
+    swap_0.wait_recv()
+    mixed[...] = totals[:, core] + mate_buf[...]
+    to_ring(lambda p: mixed.at[p], rs_buf, 1)
 
     tally = jnp.zeros((8, n_gx), F32)
     for j in range(8):
@@ -384,15 +388,15 @@
     count = dot(tally.astype(B16), jnp.ones((n_gx, PLANES), B16))
     count_v[...] = 1.0 / jnp.maximum(count, 1.0)
 
-    all_of(rs_buf, ring - 1, g_recv.at[0])
-    mine = totals[r]
-    for i in range(ring - 1):
+    all_of(rs_buf, chips - 1, g_recv.at[1])
+    mine = mixed[y_chip]
+    for i in range(chips - 1):
         mine = mine + rs_buf[i]
     part[...] = mine
 
     def swap(i, carry):
         p = (q + away(i, XGROUP)) % XGROUP
-        remote(part, ar_buf.at[i], g_send.at[1], g_recv.at[1], (p * ring + r, gy))
+        remote(part, ar_buf.at[i], g_send.at[2], g_recv.at[2], (p * ring + r, gy))
         return carry
 
     lax.fori_loop(0, XGROUP - 1, swap, 0)
@@ -400,7 +404,7 @@
         remote(new.at[:, 1, inner], new.at[:, XROWS + 1, inner], n_send.at[0], n_recv.at[0], (left, gy)),
         remote(new.at[:, XROWS, inner], new.at[:, 0, inner], n_send.at[1], n_recv.at[1], (right, gy)),
     ]
-    all_of(ar_buf, XGROUP - 1, g_recv.at[1])
+    all_of(ar_buf, XGROUP - 1, g_recv.at[2])
     for i in range(XGROUP - 1):
         mine = mine + ar_buf[i]
     mean = mine * count_v[...]
@@ -421,14 +425,16 @@
             moved = pltpu.roll(cross, hp, 1)
             gap = mean - value + jnp.where(in_c, -moved, moved)
         value = value + (relax_coarse / coarse_det) * (gap + gap_pot * pltpu.roll(gap, hp, 1))
-    sol[ring - 1] = value
-    to_ring(lambda p: sol.at[ring - 1], sol, 2)
+    sol[0, chips - 1] = value
+    to_ring(lambda p: sol.at[0, chips - 1], sol.at[0], 3)
 
     k = iota((2 * PLANES, 2 * PLANES), 0) % PLANES
     n = iota((2 * PLANES, 2 * PLANES), 1)
     widen = (k == (n // PLANES) * hp + (n % PLANES) // 2).astype(F32).astype(B16)
 
-    all_of(sol, ring - 1, g_recv.at[2])
+    all_of(sol.at[0], chips - 1, g_recv.at[3])
+    swap_1 = remote(sol.at[0], sol.at[1], g_send.at[4], g_recv.at[4], mate)
+    swap_1.wait_recv()
     solved = sol[...].reshape(n_gx, PLANES)
     both = jnp.concatenate(halves(solved), axis=1)
 
@@ -498,9 +504,11 @@
 
     for copy in ex:
         copy.wait_send()
-    all_of(rs_buf, ring - 1, g_send.at[0])
-    all_of(ar_buf, XGROUP - 1, g_send.at[1])
-    all_of(rs_buf, ring - 1, g_send.at[2])
+    swap_0.wait_send()
+    all_of(rs_buf, chips - 1, g_send.at[1])
+    all_of(ar_buf, XGROUP - 1, g_send.at[2])
+    all_of(rs_buf, chips - 1, g_send.at[3])
+    swap_1.wait_send()
 
 
 def hand_out(conc_v, pot_v, conc_o, pot_o, sem):
@@ -547,11 +555,13 @@
                 pltpu.VMEM((k_all, n_gx), B16),
                 pltpu.VMEM((16, n_gx), B16),
                 pltpu.VMEM((8, PLANES), F32),
-                pltpu.VMEM((ring, 8, PLANES), F32),
-                pltpu.VMEM((ring - 1, 8, PLANES), F32),
+                pltpu.VMEM((ring // 2, 2, 8, PLANES), F32),
+                pltpu.VMEM((ring // 2, 8, PLANES), F32),
+                pltpu.VMEM((ring // 2, 8, PLANES), F32),
+                pltpu.VMEM((max(ring // 2 - 1, 1), 8, PLANES), F32),
                 pltpu.VMEM((8, PLANES), F32),
                 pltpu.VMEM((XGROUP - 1, 8, PLANES), F32),
-                pltpu.VMEM((ring, 8, PLANES), F32),
+                pltpu.VMEM((2, ring // 2, 8, PLANES), F32),
                 pltpu.VMEM((2, 8, PLANES), F32),
                 pltpu.VMEM((2, 8, PLANES), F32),
                 pltpu.VMEM((k_all, 2 * PLANES), F32),
@@ -560,8 +570,8 @@
                 pltpu.SemaphoreType.DMA((10,)),
                 pltpu.SemaphoreType.DMA((2,)),
                 pltpu.SemaphoreType.DMA((2,)),
-                pltpu.SemaphoreType.DMA((3,)),
-                pltpu.SemaphoreType.DMA((3,)),
+                pltpu.SemaphoreType.DMA((5,)),
+                pltpu.SemaphoreType.DMA((5,)),
                 pltpu.SemaphoreType.DMA((2,)),
                 pltpu.SemaphoreType.DMA((2,)),
             ],

time: 47.8 us -> 49.6 us (1.038)
  Pallas kernels: 46.9 us -> 48.7 us
    pallas_call x1, Pallas kernels: 46.2 us -> 48 us  [on_device(): pl.pallas_call(functools.partial(kernel, n_gx, n_gy), out_shape=(out, out...]
where the time goes in v4:
time: 49.6 us; the launch traced here: 49.4 us
  Pallas kernels  48.7 us (98%)
  between operations  0.64 us (1%)
    pallas_call x1, Pallas kernels, on_device(): pl.pallas_call(functools.partial(kernel, n_gx, n_gy), out_shape=(out, out...  48 us

profile of v4, /device:TPU:1, one launch (start us, length us, event | category | flops | bytes accessed | tf_op | source)
XLA Modules:
  0.0 49.4 jit_solution(10170275773425486439)
XLA Ops:
  0.6 48.0 %shard_map.95 = (f32[4,64,128]{2,1,0:T(8,128)S(1)}, f32[4,64,128]{2,1,0:T(8,128)S(1)}) custom-call(f32[4,64,128]{2,1,0:T(8,128)} %conc_h.1, f32[4,64,128]{2,1,0:T(8,128)} %pot_h.1, f32[4,64,128]{2,1,0:T(8,128)} %mass_h.1, f32[4,64,128]{2,1,0:T(8,128)} %psrc_h.1, s32[4,64,128]{2,1,0:T(8,128)} %mask_h.1, s32[4,64,128]{2,1,0:T(8,128)} %class_h.1, f32[8]{0:T(128)} %table_h.1, ...), custom_call_target="tpu_custom_call" | custom-call | tf_op jit(solution)/shard_map/pallas_call | solution.py:534
  48.7 0.7 %shard_map.96 = (f32[4,64,128]{2,1,0:T(8,128)}, f32[4,64,128]{2,1,0:T(8,128)}) custom-call(f32[4,64,128]{2,1,0:T(8,128)S(1)} %get-tuple-element.4.conc_v, f32[4,64,128]{2,1,0:T(8,128)S(1)} %get-tuple-element.5.pot_v), custom_call_target="tpu_custom_call" | custom-call | tf_op jit(solution)/shard_map/pallas_call | solution.py:580

commit v5 on v3

--- a/solution.py
+++ b/solution.py
@@ -51,7 +51,7 @@
     w_x, w_y, w_z, w_d, w_a, new,
     r_hi, r_mid, place, pick, edge_pick, count_v,
     totals, rs_buf, part, ar_buf, sol, y_out, y_in, corr,
-    load_sem, ex_send, ex_recv, n_send, n_recv, g_send, g_recv, y_send, y_recv,
+    load_sem, ex_send, ex_recv, n_send, n_recv, g_send, g_recv, y_send, y_recv, relay,
 ):
     ring = n_gx // XGROUP
     gx = lax.axis_index("gx")
@@ -76,24 +76,28 @@
     def greet(a, b):
         pl.semaphore_signal(barrier, inc=1, device_id=(a, b), device_id_type=MESH)
 
-    def greet_ring(i, carry):
+    def near(count):
+        return [d for d in (2, count - 2, 1, count - 1) if 0 < d < count] if count > 3 else list(range(1, count))
+
+    group_near, ring_near = near(XGROUP), near(chips)
+    for d in group_near[:2]:
+        greet(((q + d) % XGROUP) * ring + r, gy)
+    for d in ring_near[:2]:
         for cross in range(2):
-            greet(q * ring + ring_at(away(i, chips), cross), gy)
-        return carry
-
-    def greet_group(i, carry):
-        greet(((q + away(i, XGROUP)) % XGROUP) * ring + r, gy)
-        return carry
-
-    lax.fori_loop(0, XGROUP - 1, greet_group, 0)
-    lax.fori_loop(0, chips - 1, greet_ring, 0)
+            greet(q * ring + ring_at(d, cross), gy)
     for a in (left, right):
         for b in (below, above):
             greet(a, b)
+    for d in group_near[2:]:
+        greet(((q + d) % XGROUP) * ring + r, gy)
+    for d in ring_near[2:]:
+        for cross in range(2):
+            greet(q * ring + ring_at(d, cross), gy)
+    for a in (left, right):
         greet(a, gy)
     for b in (below, above):
         greet(gx, b)
-    greet(q * ring + ring_at(0, 1), gy)
+    n_greet = 8 + len(group_near) + 2 * len(ring_near)
 
     def load(source, target, index):
         copy = pltpu.make_async_copy(source, target, load_sem.at[index])
@@ -121,7 +125,7 @@
         fld[2, x + 1, inner, :] = mask_v[x].astype(F32) * values
     for copy in (l_conc, l_pot, l_mass, l_psrc, l_owner):
         copy.wait()
-    pl.semaphore_wait(barrier, 8 + ring - 1 + XGROUP - 1)
+    pl.semaphore_wait(barrier, n_greet)
 
     def remote(source, target, send, recv, device):
         copy = pltpu.make_async_remote_copy(
@@ -148,6 +152,14 @@
         (src.at[:, :, tail_1], src.at[:, :, under_1], (gx, above)),
     ]
     ex = [remote(a, b, ex_send.at[i], ex_recv.at[i], dev) for i, (a, b, dev) in enumerate(plan)]
+
+    ring_relay = chips > 4
+    for i, d in enumerate((2, XGROUP - 2)):
+        pl.semaphore_signal(relay.at[i], inc=1, device_id=(((q + d) % XGROUP) * ring + r, gy), device_id_type=MESH)
+    if ring_relay:
+        for i, d in enumerate((2, chips - 2)):
+            there = q * ring + ring_at(d, 0)
+            pl.semaphore_signal(relay.at[2 + i], inc=1, device_id=(there, gy), device_id_type=MESH)
 
     half = XROWS // 2
     lanes = half * YCELLS * 2
@@ -372,6 +384,9 @@
         lax.fori_loop(0, chips - 1, body, 0)
         one(0, 1, ring - 2)
 
+    if ring_relay:
+        for i in range(2):
+            pl.semaphore_wait(relay.at[2 + i], 1)
     to_ring(lambda p: totals.at[p], rs_buf, 0)
 
     def all_of(ref, count, sem):
@@ -395,6 +410,8 @@
         remote(part, ar_buf.at[i], g_send.at[1], g_recv.at[1], (p * ring + r, gy))
         return carry
 
+    for i in range(2):
+        pl.semaphore_wait(relay.at[i], 1)
     lax.fori_loop(0, XGROUP - 1, swap, 0)
     sides = [
         remote(new.at[:, 1, inner], new.at[:, XROWS + 1, inner], n_send.at[0], n_recv.at[0], (left, gy)),
@@ -564,6 +581,7 @@
                 pltpu.SemaphoreType.DMA((3,)),
                 pltpu.SemaphoreType.DMA((2,)),
                 pltpu.SemaphoreType.DMA((2,)),
+                pltpu.SemaphoreType.REGULAR((4,)),
             ],
             compiler_params=pltpu.CompilerParams(collective_id=0, has_side_effects=True, vmem_limit_bytes=24 << 20),
         )(*(pltpu.with_memory_space_constraint(a, pltpu.HBM) for a in (conc, pot, mass, psrc, mask, classes, table, owner.T)))

time: 47.8 us -> 46.9 us (0.981)
  Pallas kernels: 46.9 us -> 46.1 us
    pallas_call x1, Pallas kernels: 46.2 us -> 45.3 us  [on_device(): pl.pallas_call(functools.partial(kernel, n_gx, n_gy), out_shape=(out, out...]
where the time goes in v5:
time: 46.9 us; the launch traced here: 46.7 us
  Pallas kernels  46.1 us (98%)
  between operations  0.64 us (1%)
    pallas_call x1, Pallas kernels, on_device(): pl.pallas_call(functools.partial(kernel, n_gx, n_gy), out_shape=(out, out...  45.3 us

profile of v5, /device:TPU:1, one launch (start us, length us, event | category | flops | bytes accessed | tf_op | source)
XLA Modules:
  0.0 46.7 jit_solution(7741918279328997728)
XLA Ops:
  0.6 45.3 %shard_map.95 = (f32[4,64,128]{2,1,0:T(8,128)S(1)}, f32[4,64,128]{2,1,0:T(8,128)S(1)}) custom-call(f32[4,64,128]{2,1,0:T(8,128)} %conc_h.1, f32[4,64,128]{2,1,0:T(8,128)} %pot_h.1, f32[4,64,128]{2,1,0:T(8,128)} %mass_h.1, f32[4,64,128]{2,1,0:T(8,128)} %psrc_h.1, s32[4,64,128]{2,1,0:T(8,128)} %mask_h.1, s32[4,64,128]{2,1,0:T(8,128)} %class_h.1, f32[8]{0:T(128)} %table_h.1, ...), custom_call_target="tpu_custom_call" | custom-call | tf_op jit(solution)/shard_map/pallas_call | solution.py:543
  46.0 0.7 %shard_map.96 = (f32[4,64,128]{2,1,0:T(8,128)}, f32[4,64,128]{2,1,0:T(8,128)}) custom-call(f32[4,64,128]{2,1,0:T(8,128)S(1)} %get-tuple-element.4.conc_v, f32[4,64,128]{2,1,0:T(8,128)S(1)} %get-tuple-element.5.pot_v), custom_call_target="tpu_custom_call" | custom-call | tf_op jit(solution)/shard_map/pallas_call | solution.py:588

commit v6 on v5

--- a/solution.py
+++ b/solution.py
@@ -50,7 +50,7 @@
     fld, src, mask_v, class_v, owner_v, table,
     w_x, w_y, w_z, w_d, w_a, new,
     r_hi, r_mid, place, pick, edge_pick, count_v,
-    totals, rs_buf, part, ar_buf, sol, y_out, y_in, corr,
+    totals, rs_buf, part, ar_buf, sol, y_out, y_in, corr, solve_v,
     load_sem, ex_send, ex_recv, n_send, n_recv, g_send, g_recv, y_send, y_recv, relay,
 ):
     ring = n_gx // XGROUP
@@ -399,6 +399,33 @@
     count = dot(tally.astype(B16), jnp.ones((n_gx, PLANES), B16))
     count_v[...] = 1.0 / jnp.maximum(count, 1.0)
 
+    hp = PLANES // 2
+    z = iota((PLANES, PLANES), 1)
+    in_c = z < hp
+    no_up = (z % hp) == hp - 1
+    no_dn = (z % hp) == 0
+    gap_pot = jnp.where(in_c, -2.0 * coarse_flux, 1.0 + 2.0 * coarse_bend)
+    unit = (iota((PLANES, PLANES), 0) == z).astype(F32)
+    value = jnp.zeros((PLANES, PLANES), F32)
+    for sweep_at in range(CSWEEP):
+        gap = unit
+        if sweep_at:
+            around = jnp.where(no_up, 0.0, pltpu.roll(value, PLANES - 1, 1)) + jnp.where(no_dn, 0.0, pltpu.roll(value, 1, 1))
+            bend = 2.0 * value - around
+            cross = jnp.where(in_c, value + coarse_bend * bend, coarse_flux * bend)
+            moved = pltpu.roll(cross, hp, 1)
+            gap = unit - value + jnp.where(in_c, -moved, moved)
+        value = value + (relax_coarse / coarse_det) * (gap + gap_pot * pltpu.roll(gap, hp, 1))
+    k = iota((PLANES, 2 * PLANES), 0)
+    n = iota((PLANES, 2 * PLANES), 1)
+    widen = (k == (n // PLANES) * hp + (n % PLANES) // 2).astype(F32).astype(B16)
+    for i, piece in enumerate(halves(value)):
+        solve_v[i] = dot(piece, widen).astype(B16)
+
+    def correct(high_mid):
+        high, rest = high_mid[:, :PLANES], high_mid[:, PLANES:]
+        return dot(high, solve_v[0]) + (dot(rest, solve_v[0]) + dot(high, solve_v[1]))
+
     all_of(rs_buf, ring - 1, g_recv.at[0])
     mine = totals[r]
     for i in range(ring - 1):
@@ -422,28 +449,8 @@
         mine = mine + ar_buf[i]
     mean = mine * count_v[...]
 
-    hp = PLANES // 2
-    z = iota((8, PLANES), 1)
-    in_c = z < hp
-    no_up = (z % hp) == hp - 1
-    no_dn = (z % hp) == 0
-    gap_pot = jnp.where(in_c, -2.0 * coarse_flux, 1.0 + 2.0 * coarse_bend)
-    value = jnp.zeros((8, PLANES), F32)
-    for step in range(CSWEEP):
-        gap = mean
-        if step:
-            around = jnp.where(no_up, 0.0, pltpu.roll(value, PLANES - 1, 1)) + jnp.where(no_dn, 0.0, pltpu.roll(value, 1, 1))
-            bend = 2.0 * value - around
-            cross = jnp.where(in_c, value + coarse_bend * bend, coarse_flux * bend)
-            moved = pltpu.roll(cross, hp, 1)
-            gap = mean - value + jnp.where(in_c, -moved, moved)
-        value = value + (relax_coarse / coarse_det) * (gap + gap_pot * pltpu.roll(gap, hp, 1))
-    sol[ring - 1] = value
+    sol[ring - 1] = mean
     to_ring(lambda p: sol.at[ring - 1], sol, 2)
-
-    k = iota((2 * PLANES, 2 * PLANES), 0) % PLANES
-    n = iota((2 * PLANES, 2 * PLANES), 1)
-    widen = (k == (n // PLANES) * hp + (n % PLANES) // 2).astype(F32).astype(B16)
 
     all_of(sol, ring - 1, g_recv.at[2])
     solved = sol[...].reshape(n_gx, PLANES)
@@ -456,7 +463,7 @@
         remote(y_out.at[0], y_in.at[1], y_send.at[0], y_recv.at[0], (gx, below)),
         remote(y_out.at[1], y_in.at[0], y_send.at[1], y_recv.at[1], (gx, above)),
     ]
-    corr[...] = dot(dot(pick[...], both).astype(B16), widen)
+    corr[...] = correct(dot(pick[...], both).astype(B16))
 
     for copy in sides:
         copy.wait()
@@ -498,7 +505,7 @@
 
     for copy in ends:
         copy.wait()
-    y_fine = dot(jnp.concatenate(halves(y_in[...].reshape(16, PLANES)), axis=1), widen)
+    y_fine = correct(jnp.concatenate(halves(y_in[...].reshape(16, PLANES)), axis=1))
     inside = (jnp.where(gy == 0, 0.0, 1.0), jnp.where(gy == n_gy - 1, 0.0, 1.0))
     for side in range(2):
         row, out_row = (first, 0) if side == 0 else (last - 1, YCELLS - 1)
@@ -572,6 +579,7 @@
                 pltpu.VMEM((2, 8, PLANES), F32),
                 pltpu.VMEM((2, 8, PLANES), F32),
                 pltpu.VMEM((k_all, 2 * PLANES), F32),
+                pltpu.VMEM((2, PLANES, 2 * PLANES), B16),
                 pltpu.SemaphoreType.DMA((8,)),
                 pltpu.SemaphoreType.DMA((10,)),
                 pltpu.SemaphoreType.DMA((10,)),

time: 46.9 us -> 46.4 us (0.989)
  Pallas kernels: 46.1 us -> 45.6 us
    pallas_call x1, Pallas kernels: 45.3 us -> 44.9 us  [on_device(): pl.pallas_call(functools.partial(kernel, n_gx, n_gy), out_shape=(out, out...]
where the time goes in v6:
time: 46.4 us; the launch traced here: 46.2 us
  Pallas kernels  45.6 us (98%)
  between operations  0.64 us (1%)
    pallas_call x1, Pallas kernels, on_device(): pl.pallas_call(functools.partial(kernel, n_gx, n_gy), out_shape=(out, out...  44.9 us

profile of v6, /device:TPU:1, one launch (start us, length us, event | category | flops | bytes accessed | tf_op | source)
XLA Modules:
  0.0 46.2 jit_solution(5086235630696121973)
XLA Ops:
  0.6 44.9 %shard_map.95 = (f32[4,64,128]{2,1,0:T(8,128)S(1)}, f32[4,64,128]{2,1,0:T(8,128)S(1)}) custom-call(f32[4,64,128]{2,1,0:T(8,128)} %conc_h.1, f32[4,64,128]{2,1,0:T(8,128)} %pot_h.1, f32[4,64,128]{2,1,0:T(8,128)} %mass_h.1, f32[4,64,128]{2,1,0:T(8,128)} %psrc_h.1, s32[4,64,128]{2,1,0:T(8,128)} %mask_h.1, s32[4,64,128]{2,1,0:T(8,128)} %class_h.1, f32[8]{0:T(128)} %table_h.1, ...), custom_call_target="tpu_custom_call" | custom-call | tf_op jit(solution)/shard_map/pallas_call | solution.py:550
  45.5 0.7 %shard_map.96 = (f32[4,64,128]{2,1,0:T(8,128)}, f32[4,64,128]{2,1,0:T(8,128)}) custom-call(f32[4,64,128]{2,1,0:T(8,128)S(1)} %get-tuple-element.4.conc_v, f32[4,64,128]{2,1,0:T(8,128)S(1)} %get-tuple-element.5.pot_v), custom_call_target="tpu_custom_call" | custom-call | tf_op jit(solution)/shard_map/pallas_call | solution.py:596

commit v7 on v6

--- a/solution.py
+++ b/solution.py
@@ -139,17 +139,19 @@
     head_1, tail_1 = pl.ds(first, 1), pl.ds(last - 1, 1)
     over_1, under_1 = pl.ds(last, 1), pl.ds(first - 1, 1)
     rows = pl.ds(1, XROWS)
+    out_row, out_far, out_dev = 1 + (XROWS - 1) * core, (XROWS + 1) * (1 - core), (gx + n_gx + 2 * core - 1) % n_gx
+    in_row, in_far, in_dev = XROWS - (XROWS - 1) * core, (XROWS + 1) * core, (gx + n_gx + 1 - 2 * core) % n_gx
     plan = [
+        (fld.at[:, out_row, inner], fld.at[:, out_far, inner], (out_dev, gy)),
         (fld.at[:, 1, head_1], fld.at[:, XROWS + 1, over_1], (left, below)),
         (fld.at[:, 1, tail_1], fld.at[:, XROWS + 1, under_1], (left, above)),
         (fld.at[:, XROWS, head_1], fld.at[:, 0, over_1], (right, below)),
         (fld.at[:, XROWS, tail_1], fld.at[:, 0, under_1], (right, above)),
-        (fld.at[:, 1, inner], fld.at[:, XROWS + 1, inner], (left, gy)),
-        (fld.at[:, XROWS, inner], fld.at[:, 0, inner], (right, gy)),
         (fld.at[:, rows, head], fld.at[:, rows, over], (gx, below)),
         (fld.at[:, rows, tail], fld.at[:, rows, under], (gx, above)),
         (src.at[:, :, head_1], src.at[:, :, over_1], (gx, below)),
         (src.at[:, :, tail_1], src.at[:, :, under_1], (gx, above)),
+        (fld.at[:, in_row, inner], fld.at[:, in_far, inner], (in_dev, gy)),
     ]
     ex = [remote(a, b, ex_send.at[i], ex_recv.at[i], dev) for i, (a, b, dev) in enumerate(plan)]
 
@@ -528,10 +530,10 @@
 
 
 def hand_out(conc_v, pot_v, conc_o, pot_o, sem):
-    copies = [
-        pltpu.make_async_copy(conc_v, conc_o, sem.at[0]),
-        pltpu.make_async_copy(pot_v, pot_o, sem.at[1]),
-    ]
+    copies = []
+    for x in range(XROWS):
+        copies.append(pltpu.make_async_copy(conc_v.at[x], conc_o.at[x], sem.at[2 * x]))
+        copies.append(pltpu.make_async_copy(pot_v.at[x], pot_o.at[x], sem.at[2 * x + 1]))
     for copy in copies:
         copy.start()
     for copy in copies:
@@ -598,7 +600,7 @@
             out_shape=(out, out),
             in_specs=[pl.BlockSpec(memory_space=pltpu.VMEM)] * 2,
             out_specs=(any_spec, any_spec),
-            scratch_shapes=[pltpu.SemaphoreType.DMA((2,))],
+            scratch_shapes=[pltpu.SemaphoreType.DMA((2 * XROWS,))],
             compiler_params=pltpu.CompilerParams(vmem_limit_bytes=1 << 20),
         )(*held)
 

time: 46.4 us -> 47.5 us (1.024)
  Pallas kernels: 45.6 us -> 46.7 us
    pallas_call x1, Pallas kernels: 44.9 us -> 45.9 us  [on_device(): pl.pallas_call(functools.partial(kernel, n_gx, n_gy), out_shape=(out, out...]
where the time goes in v7:
time: 47.5 us; the launch traced here: 47.3 us
  Pallas kernels  46.7 us (98%)
  between operations  0.64 us (1%)
    pallas_call x1, Pallas kernels, on_device(): pl.pallas_call(functools.partial(kernel, n_gx, n_gy), out_shape=(out, out...  45.9 us

profile of v7, /device:TPU:1, one launch (start us, length us, event | category | flops | bytes accessed | tf_op | source)
XLA Modules:
  0.0 47.3 jit_solution(2219624825244878631)
XLA Ops:
  0.6 45.9 %shard_map.95 = (f32[4,64,128]{2,1,0:T(8,128)S(1)}, f32[4,64,128]{2,1,0:T(8,128)S(1)}) custom-call(f32[4,64,128]{2,1,0:T(8,128)} %conc_h.1, f32[4,64,128]{2,1,0:T(8,128)} %pot_h.1, f32[4,64,128]{2,1,0:T(8,128)} %mass_h.1, f32[4,64,128]{2,1,0:T(8,128)} %psrc_h.1, s32[4,64,128]{2,1,0:T(8,128)} %mask_h.1, s32[4,64,128]{2,1,0:T(8,128)} %class_h.1, f32[8]{0:T(128)} %table_h.1, ...), custom_call_target="tpu_custom_call" | custom-call | tf_op jit(solution)/shard_map/pallas_call | solution.py:552
  46.5 0.8 %shard_map.96 = (f32[4,64,128]{2,1,0:T(8,128)}, f32[4,64,128]{2,1,0:T(8,128)}) custom-call(f32[4,64,128]{2,1,0:T(8,128)S(1)} %get-tuple-element.4.conc_v, f32[4,64,128]{2,1,0:T(8,128)S(1)} %get-tuple-element.5.pot_v), custom_call_target="tpu_custom_call" | custom-call | tf_op jit(solution)/shard_map/pallas_call | solution.py:598
